TPU v7x, 32 devices: a whole 2x2x4 slice. The times are simulated.
32 devices in a mesh: row: 4 (over z), col: 2 (over x), feat: 4 (over y, core).
Axes of the slice: x: 2, y: 2, z: 4, core: 2. Of those that a mesh axis runs over, the one named last changes fastest.
Arguments:
- snapshots: bfloat16 [512, 32768], P(('row', 'col'), 'feat'), may hold values from -6 to 6
- start_block: float32 [512, 32], P('row'), may hold values from -6 to 6
Outputs:
- eigen_basis: float32 [512, 32], P('row')
All inputs are finite; a program needn't handle non-finite values.
Results may differ from a plain program's by a relative error of at most 0.0003.
Values may be sent and summed in bfloat16 or wider, within the bound.
No kernel may reach another device: no remote copies, remote signals or barrier semaphores. Data moves between devices by JAX's collectives and lax.ppermute only.
A program may use at most 64 MiB of HBM per device.

v0:
```python
import functools
import math

import jax
import jax.numpy as jnp
from jax import lax
from jax.experimental import pallas as pl
from jax.experimental.pallas import tpu as pltpu
from jax.sharding import PartitionSpec as P


LAGS = 128
ITERS = 6
TILE = 128
PANEL = 16


kernel_spread = 0.25
highest = lax.Precision.HIGHEST
f32 = jnp.float32
bf16 = jnp.bfloat16


def broadcast(x, axis, root):
    mine = lax.axis_index(axis) == root
    return lax.psum(jnp.where(mine, x, jnp.zeros_like(x)), axis)


def shifted(x, axis, by):
    length = lax.axis_size(axis)
    pairs = [(i, i + by) for i in range(length) if 0 <= i + by < length]
    return lax.ppermute(x, axis, pairs)


def diagonal_window(extended, lag_count):
    running = None
    partial_sum = extended
    levels = lag_count.bit_length()
    for level in range(levels):
        stride = 1 << level
        if lag_count & stride:
            running = partial_sum
        if level + 1 < levels:
            partial_sum = partial_sum[:-stride, :-stride] + partial_sum[stride:, stride:]
    return running


def orthonormal(product, gram_sum):
    factor = jnp.linalg.cholesky(gram_sum)
    return jax.scipy.linalg.solve_triangular(factor, product.T, lower=True).T


def square_norms(fields):
    widened = fields.astype(f32)
    return jnp.sum(widened * widened, axis=1)


def spread_body(points, snapshots, start_block):
    row_total = lax.axis_size("row")
    col_total = lax.axis_size("col")
    row_place = lax.axis_index("row")
    col_place = lax.axis_index("col")
    shard_rows = snapshots.shape[0]
    block_rows = shard_rows * col_total
    pairing = row_total // col_total
    block_cols = block_rows * pairing
    own_rows = lax.all_gather(snapshots, "col", axis=0, tiled=True)
    own_norms = square_norms(own_rows)
    members = []
    for member in range(pairing):
        members.append(broadcast(own_rows, "row", pairing * col_place + member))
    col_data = jnp.concatenate(members, axis=0)
    col_norms = square_norms(col_data)
    products = lax.dot_general(
        own_rows, col_data, (((1,), (1,)), ((), ())), preferred_element_type=f32
    )
    partial_dist = own_norms[:, None] + col_norms[None, :] - 2.0 * products
    distance = lax.psum(partial_dist, "feat")
    rim_width = LAGS - 1
    top_rim = shifted(distance[block_rows - rim_width :], "row", 1)
    upper = jnp.concatenate([top_rim, distance], axis=0)
    left_side = shifted(upper[:, block_cols - rim_width :], "col", 1)
    extended = jnp.concatenate([left_side, upper], axis=1)
    lagged = diagonal_window(extended, LAGS)
    row_ids = row_place * block_rows + lax.broadcasted_iota(jnp.int32, (block_rows, block_cols), 0)
    col_ids = col_place * block_cols + lax.broadcasted_iota(jnp.int32, (block_rows, block_cols), 1)
    counts = jnp.minimum(jnp.minimum(row_ids, col_ids), rim_width) + 1
    kernel = jnp.exp(-(lagged / (counts.astype(f32) * points)) / kernel_spread)
    row_degree = lax.psum(jnp.sum(kernel, axis=1), "col")
    every_degree = lax.all_gather(row_degree, "row", axis=0, tiled=True)
    col_degree = lax.dynamic_slice_in_dim(every_degree, col_place * block_cols, block_cols)
    markov = kernel * lax.rsqrt(row_degree)[:, None] * lax.rsqrt(col_degree)[None, :]
    basis = start_block
    for _ in range(ITERS // 2):
        product = lax.dot_general(
            markov,
            basis,
            (((0,), (0,)), ((), ())),
            precision=highest,
            preferred_element_type=f32,
        )
        summed_cols = lax.psum(product, "row")
        row_product = jnp.dot(markov, summed_cols, precision=highest, preferred_element_type=f32)
        summed_rows = lax.psum(row_product, "col")
        local_gram = jnp.dot(
            summed_rows.T, summed_rows, precision=highest, preferred_element_type=f32
        )
        gram_rows = lax.psum(local_gram, "row")
        basis = orthonormal(summed_rows, gram_rows)
    return basis * math.sqrt(row_total * block_rows)


def any_spec():
    return pl.BlockSpec(memory_space=pl.ANY)


def vmem_spec():
    return pl.BlockSpec(memory_space=pltpu.VMEM)


def near(x):
    return pltpu.with_memory_space_constraint(x, pltpu.VMEM)


def xor_permute(x, axis, mask):
    return lax.ppermute(x, axis, [(i, i ^ mask) for i in range(lax.axis_size(axis))])


def quad_permute(x, mask):
    cols, feats = lax.axis_size("col"), lax.axis_size("feat")
    pairs = []
    for col in range(cols):
        for feat in range(feats):
            there = (col ^ (mask >> 1)) * feats + (feat ^ ((mask & 1) * (feats // 2)))
            pairs.append((col * feats + feat, there))
    return lax.ppermute(x, ("col", "feat"), pairs)


def packed_blocks(tiles):
    full = [(b, c) for b in range(tiles) for c in range(b)]
    return full, [(b, b + 1) for b in range(0, tiles, 2)]


def ring_steps(rows, cols):
    shifts = [rows // 2, 1, rows - 1]
    steps = [(a, (n + turn) % cols) for turn in range(cols) for n, a in enumerate(shifts)]
    return [(0, 0)] + steps + [(0, mask) for mask in range(1, cols)]


def device_places():
    row, col, feat = lax.axis_index("row"), lax.axis_index("col"), lax.axis_index("feat")
    return feat & 1, col * 2 + (feat >> 1), row, col


def cut_kernel(steps, rows_total, cols, width, x_ref, *refs):
    members = len(steps)
    outs, sems = refs[:members], refs[members]
    parts = sems.shape[0] // members
    rows_each = x_ref.shape[0] // parts
    _, _, row, col = device_places()
    copies = []
    for step, (shift, mask) in enumerate(steps):
        there = lax.rem(row + shift, rows_total) * cols + (col ^ mask)
        begin = pl.multiple_of(there * width, TILE)
        for part in range(parts):
            rows = slice(part * rows_each, (part + 1) * rows_each)
            copies.append(
                pltpu.make_async_copy(
                    x_ref.at[rows, pl.ds(begin, width)],
                    outs[step].at[rows, :],
                    sems.at[step * parts + part],
                )
            )
    for copy in copies:
        copy.start()
    for copy in copies:
        copy.wait()


def pieces_of(whole):
    high = whole.astype(bf16)
    rest = whole - high.astype(f32)
    middle = rest.astype(bf16)
    return high, middle, (rest - middle.astype(f32)).astype(bf16)


def add_dots(weights, pieces):
    total = None
    for piece in pieces:
        term = jnp.dot(weights, piece, preferred_element_type=f32)
        total = term if total is None else total + term
    return total


def gram_kernel(steps, rows_total, cols, rows, *refs):
    members = len(steps)
    received, starts = refs[:members], refs[members : members + 2]
    keep_ref, send_ref, begin_ref, data_ref = refs[members + 2 :]
    half, _, row_place, col_place = device_places()
    for step, (shift, mask) in enumerate(steps):
        source = lax.rem(row_place + (rows_total - shift), rows_total) * cols + (col_place ^ mask)
        data_ref[pl.ds(pl.multiple_of(source * rows, rows), rows), :] = received[step][...]
    vecs = starts[0].shape[0]
    for mask in range(2):
        begin_ref[mask * vecs : (mask + 1) * vecs, :] = starts[mask][...]
    tiles = members * rows // TILE
    sub = lax.broadcasted_iota(jnp.int32, (TILE, TILE), 0)
    lane = lax.broadcasted_iota(jnp.int32, (TILE, TILE), 1)
    anti = sub + lane == TILE - 1
    flip = anti.astype(bf16)
    contract = (((1,), (1,)), ((), ()))
    strips, row_norms, col_norms = [], [], []
    for b in range(tiles):
        mirror = tiles - 1 - b
        block = data_ref[mirror * TILE : (mirror + 1) * TILE, :]
        turned = jnp.dot(flip, block, preferred_element_type=f32).astype(bf16)
        prods = lax.dot_general(
            turned, data_ref[: (mirror + 1) * TILE, :], contract, preferred_element_type=f32
        )
        strips.append(prods)
        own = jnp.where(anti, prods[:, mirror * TILE :], 0.0)
        row_norms.append(jnp.sum(own, axis=1, keepdims=True))
        col_norms.append(jnp.sum(own, axis=0, keepdims=True))
    norms = jnp.concatenate(col_norms[::-1], axis=1)
    late = (sub + lane >= TILE - 1).astype(bf16)
    early = (sub + lane < TILE - 1).astype(bf16)
    skewed = []
    for b in range(tiles):
        span = (tiles - b) * TILE
        dist = row_norms[b] + norms[:, :span] - 2.0 * strips[b]
        dist = pltpu.roll(dist, 0, 1, stride=1, stride_axis=0)
        head = jnp.where(lane >= sub, dist[:, :TILE], 0.0)
        if span > TILE:
            head = jnp.concatenate([head, dist[:, TILE:]], axis=1)
        skewed.append(pieces_of(head))
    lags = []
    for block in range(tiles):
        b = tiles - 1 - block
        span = (block + 1) * TILE
        lagged = add_dots(late, skewed[b])
        if block > 0:
            more = add_dots(early, skewed[b + 1])
            lagged = jnp.concatenate([lagged[:, :TILE], lagged[:, TILE:] + more], axis=1)
        lags.append(pltpu.roll(lagged, (1 + span - TILE) % span, 1, stride=1, stride_axis=0))
    full, pairs = packed_blocks(tiles)
    values = [lags[b][:, c * TILE : (c + 1) * TILE] for b, c in full]
    for one, two in pairs:
        values.append(jnp.where(lane < sub, lags[one][:, -TILE:], lags[two][:, -TILE:].T))
    count = len(values) // 2
    for slot in range(count):
        rows = slice(slot * TILE, (slot + 1) * TILE)
        keep_ref[rows, :] = jnp.where(half == 0, values[slot], values[count + slot])
        send_ref[rows, :] = jnp.where(half == 0, values[count + slot], values[slot])


def quarter_kernel(chunk, keep_ref, got_ref, *outs):
    quad = device_places()[1]
    for mask in range(4):
        rows = pl.ds(pl.multiple_of((quad ^ mask) * chunk, 8), chunk)
        outs[mask][...] = keep_ref[rows, :] + got_ref[rows, :]


def split(x):
    high = x.astype(bf16)
    return high, (x - high.astype(f32)).astype(bf16)


def split_dot(a, b, contract=(((1,), (0,)), ((), ()))):
    a_high, a_low = split(a)
    b_high, b_low = split(b)
    rows = a.shape[0]
    stacked = jnp.concatenate([a_high, a_low], axis=0)
    first = lax.dot_general(stacked, b_high, contract, preferred_element_type=f32)
    second = lax.dot_general(a_high, b_low, contract, preferred_element_type=f32)
    return first[:rows] + (first[rows:] + second)


def inverse_factor(small):
    size = small.shape[0]
    sub = lax.broadcasted_iota(jnp.int32, (size, size), 0)
    lane = lax.broadcasted_iota(jnp.int32, (size, size), 1)
    eye = (sub == lane).astype(f32)
    rest = jnp.concatenate([small, eye], axis=1)
    done = []
    for first in range(0, size, PANEL):
        wide = rest.shape
        below = lax.broadcasted_iota(jnp.int32, wide, 0)
        columns = [
            jnp.broadcast_to(rest[:, first + a : first + a + 1], wide) for a in range(PANEL)
        ]
        for a in range(min(PANEL, size - 1 - first)):
            scale = columns[a] * (1.0 / columns[a][a : a + 1, :])
            scale = jnp.where(below > a, scale, 0.0)
            for b in range(a + 1, PANEL):
                columns[b] = columns[b] - scale * columns[b][a : a + 1, :]
            rest = rest - scale * rest[a : a + 1, :]
        done.append(rest[:PANEL, :])
        rest = rest[PANEL:, :]
    work = jnp.concatenate(done, axis=0)
    pivots = jnp.sum(work[:, :size] * eye, axis=1, keepdims=True)
    begin = jnp.sum(small * eye, axis=1, keepdims=True)
    return work[:, size:] * lax.rsqrt(pivots), jnp.min(pivots / begin)


def finish_kernel(points, tiles, chunk, snaps, *refs):
    pieces, begins = refs[:8], refs[8:10]
    out_ref, packed_ref, high_ref, low_ref, wide_ref = refs[10:]
    half, quad, row_place, _ = device_places()
    for side in range(2):
        for mask in range(4):
            begin = pl.multiple_of((half ^ side) * (4 * chunk) + (quad ^ mask) * chunk, 8)
            packed_ref[pl.ds(begin, chunk), :] = pieces[side * 4 + mask][...]
    rows = snaps // 4
    sub = lax.broadcasted_iota(jnp.int32, (TILE, TILE), 0)
    lane = lax.broadcasted_iota(jnp.int32, (TILE, TILE), 1)
    full, pairs = packed_blocks(tiles)

    def factor(counts):
        return -1.0 / (counts.astype(f32) * (points * kernel_spread))

    def keep(value, block, c):
        high, low = split(value)
        high_ref[block * TILE : (block + 1) * TILE, c * TILE : (c + 1) * TILE] = high
        low_ref[block * TILE : (block + 1) * TILE, c * TILE : (c + 1) * TILE] = low

    for at, (block, c) in enumerate(full):
        columns = c * TILE + lane[:1, :]
        scale = factor(jnp.minimum(columns, LAGS - 1) + 1)
        value = jnp.exp(packed_ref[at * TILE : (at + 1) * TILE, :] * scale)
        keep(value, block, c)
        keep(value.T, c, block)
    for at, (one, two) in enumerate(pairs):
        shared = packed_ref[(len(full) + at) * TILE : (len(full) + at + 1) * TILE, :]
        swapped = shared.T
        for block, lagged in (
            (one, jnp.where(lane < sub, shared, swapped)),
            (two, jnp.where(lane > sub, shared, swapped)),
        ):
            counts = jnp.minimum(block * TILE + jnp.minimum(sub, lane), LAGS - 1) + 1
            lagged = jnp.where(lane == sub, 0.0, lagged)
            keep(jnp.exp(lagged * factor(counts)), block, block)
    ones = jnp.ones((16, snaps), bf16)
    degrees = jnp.dot(ones, high_ref[...], preferred_element_type=f32)
    degrees = degrees + jnp.dot(ones, low_ref[...], preferred_element_type=f32)
    inverse = 1.0 / degrees[0:1, :]
    scales = lax.sqrt(inverse)
    vecs = begins[0].shape[0] // 2
    for mask in range(4):
        begin = pl.multiple_of((row_place ^ mask) * rows, TILE)
        half_rows = slice(mask % 2 * vecs, (mask % 2 + 1) * vecs)
        wide_ref[:, pl.ds(begin, rows)] = begins[mask // 2][half_rows, :]
    start = wide_ref[...]

    def apply(x):
        x_high, x_low = split(x)
        stacked = jnp.concatenate([x_high, x_low], axis=0)
        first = jnp.dot(stacked, high_ref[...], preferred_element_type=f32)
        second = jnp.dot(x_high, low_ref[...], preferred_element_type=f32)
        return first[:vecs] + (first[vecs:] + second)

    across = (((1,), (1,)), ((), ()))

    def rounds(x, least, times):
        x = apply(x * scales)
        for _ in range(times - 1):
            x = apply(x * inverse)
        x = x * scales
        factor, ratio = inverse_factor(split_dot(x, x, across))
        return split_dot(factor, x), jnp.minimum(least, ratio)

    def loop(times):
        return lax.fori_loop(
            0,
            ITERS // times,
            lambda _, c: rounds(c[0], c[1], times),
            (start, f32(1.0)),
            unroll=times == 3,
        )

    basis, least = loop(3)
    wide_ref[...] = basis

    @pl.when(jnp.logical_not(least > 1e-4))
    def _():
        wide_ref[...] = loop(1)[0]

    basis = wide_ref[...]
    eye_sub = lax.broadcasted_iota(jnp.int32, (vecs, vecs), 0)
    eye_lane = lax.broadcasted_iota(jnp.int32, (vecs, vecs), 1)
    error = split_dot(basis, basis, across) - (eye_sub == eye_lane).astype(f32)
    weight = jnp.where(eye_sub > eye_lane, 1.0, jnp.where(eye_sub == eye_lane, 0.5, 0.0))
    wide_ref[...] = (basis - split_dot(error * weight, basis)) * math.sqrt(snaps)
    out_ref[...] = wide_ref[:, pl.ds(pl.multiple_of(row_place * rows, TILE), rows)]


def packed_body(points, snapshots, start_block):
    return packed_plan(points, snapshots, start_block)


def packed_plan(points, snapshots, start_block):
    cols = lax.axis_size("col")
    rows_total = lax.axis_size("row")
    members = rows_total * cols
    shard_rows, shard_points = snapshots.shape
    width = shard_points // members
    snaps = shard_rows * members
    tiles = snaps // TILE
    vecs = start_block.shape[1]
    steps = ring_steps(rows_total, cols)
    cuts = {}
    for group in ((1,), tuple(range(2, members)) + (0,)):
        chosen = [steps[step] for step in group]
        outs = pl.pallas_call(
            functools.partial(cut_kernel, chosen, rows_total, cols, width),
            out_shape=[pltpu.VMEM((shard_rows, width), bf16)] * len(group),
            in_specs=[any_spec()],
            out_specs=[vmem_spec()] * len(group),
            scratch_shapes=[pltpu.SemaphoreType.DMA((len(group) * (4 if len(group) == 1 else 1),))],
            name="cut",
        )(snapshots)
        cuts.update(zip(group, outs))
    received = [cuts[0]]
    for step in range(1, members):
        shift, mask = steps[step]
        pairs = []
        for row in range(rows_total):
            for col in range(cols):
                there = (row + shift) % rows_total * cols + (col ^ mask)
                pairs.append((row * cols + col, there))
        received.append(lax.ppermute(cuts[step], ("row", "col"), pairs))
    turned = start_block.T
    starts = [turned, xor_permute(turned, "row", 1)]

    full, shared = packed_blocks(tiles)
    total = (len(full) + len(shared)) * TILE
    side = total // 2
    chunk = side // 4
    keep, send, begin = pl.pallas_call(
        functools.partial(gram_kernel, steps, rows_total, cols, shard_rows),
        out_shape=[pltpu.VMEM((side, TILE), f32)] * 2 + [pltpu.VMEM((2 * vecs, snaps // rows_total), f32)],
        in_specs=[vmem_spec()] * (members + 2),
        out_specs=[vmem_spec()] * 3,
        scratch_shapes=[pltpu.VMEM((snaps, width), bf16)],
        name="gram",
    )(*[near(x) for x in received + starts])
    got = xor_permute(send, "feat", 1)
    begins = [begin, xor_permute(begin, "row", 2)]
    quarters = pl.pallas_call(
        functools.partial(quarter_kernel, chunk),
        out_shape=[pltpu.VMEM((chunk, TILE), f32)] * 4,
        in_specs=[vmem_spec()] * 2,
        out_specs=[vmem_spec()] * 4,
        name="quarter",
    )(near(keep), near(got))
    mine = quarters[0]
    arrived = {}
    for mask in (3, 1, 2):
        arrived[mask] = quad_permute(quarters[mask], mask)
    mine = (mine + arrived[3]) + (arrived[1] + arrived[2])
    others = {mask: xor_permute(mine, "row", mask) for mask in (1, 3, 2)}
    mine = (mine + others[1]) + (others[3] + others[2])
    pieces = [mine] + [quad_permute(mine, mask) for mask in range(1, 4)]
    pieces = pieces + [xor_permute(piece, "feat", 1) for piece in pieces]
    basis = pl.pallas_call(
        functools.partial(finish_kernel, float(points), tiles, chunk, snaps),
        out_shape=jax.ShapeDtypeStruct((vecs, snaps // rows_total), f32),
        in_specs=[vmem_spec()] * 10,
        out_specs=vmem_spec(),
        scratch_shapes=[
            pltpu.VMEM((total, TILE), f32),
            pltpu.VMEM((snaps, snaps), bf16),
            pltpu.VMEM((snaps, snaps), bf16),
            pltpu.VMEM((vecs, snaps), f32),
        ],
        name="finish",
    )(*[near(x) for x in pieces + begins])
    return basis.T


def solution(mesh):
    sizes = dict(mesh.shape)
    placed = (P(("row", "col"), "feat"), P("row", None))

    def run(snapshots, start_block):
        snaps, points = snapshots.shape
        members = sizes["row"] * sizes["col"]
        tiles = snaps // TILE
        packs = (
            sizes["row"] == 4
            and sizes["col"] == 2
            and sizes["feat"] == 4
            and snaps % (TILE * sizes["row"]) == 0
            and points % (TILE * members * sizes["feat"]) == 0
            and (tiles * tiles // 2) % 2 == 0
            and snaps <= 1024
        )
        body = packed_body if packs else spread_body
        mapped = jax.shard_map(
            functools.partial(body, points),
            mesh=mesh,
            in_specs=placed,
            out_specs=P("row", None),
            check_vma=False,
        )
        return mapped(snapshots, start_block)

    return run
```

profile of v0, /device:TPU:0, one launch (start us, length us, event | category | flops | bytes accessed | tf_op | source)
XLA Modules:
  0.0 65.8 jit_solution(10105345893911607033)
XLA Ops:
  0.0 0.8 %cut.3 = bf16[64,1024]{1,0:T(8,128)(2,1)S(1)} custom-call(bf16[64,8192]{1,0:T(8,128)(2,1)} %x_ref.3), custom_call_target="tpu_custom_call" | custom-call | tf_op jit(solution)/shard_map/cut/pallas_call | solution.py:413
  0.8 0.0 copy-start
  0.9 4.1 %collective-permute-start = (bf16[64,1024]{1,0:T(8,128)(2,1)S(1)}, bf16[64,1024]{1,0:T(8,128)(2,1)S(1)}, u32[]{:S(2)}, u32[]{:S(2)}) collective-permute-start(bf16[64,1024]{1,0:T(8,128)(2,1)S(1)} %cut.3), channel_id=1, source_target_pairs={{0,16},{4,20},{8,24},{12,28},{16,0},{20,4},{24,8},{28,12},{1,17},{... | collective-permute-start | bytes 393224 | tf_op jit(solution)/shard_map/ppermute | solution.py:430
  5.0 1.3 %cut.2 = (bf16[64,1024]{1,0:T(8,128)(2,1)S(1)}, bf16[64,1024]{1,0:T(8,128)(2,1)S(1)}, bf16[64,1024]{1,0:T(8,128)(2,1)S(1)}, bf16[64,1024]{1,0:T(8,128)(2,1)S(1)}...) custom-call(bf16[64,8192]{1,0:T(8,128)(2,1)} %x_ref.3), custom_call_target="tpu_custom_call" | custom-call | tf_op jit(solution)/shard_map/cut/pallas_call | solution.py:413
  6.3 2.6 %collective-permute-start.1 = (bf16[64,1024]{1,0:T(8,128)(2,1)S(1)}, bf16[64,1024]{1,0:T(8,128)(2,1)S(1)}, u32[]{:S(2)}, u32[]{:S(2)}) collective-permute-start(bf16[64,1024]{1,0:T(8,128)(2,1)S(1)} %get-tuple-element.20), channel_id=1, source_target_pairs={{0,12},{4,8},{8,20},{12,16},{16,28},{20,24},{24,4},{28,0},{1,13},{... | collective-permute-start | bytes 393224 | tf_op jit(solution)/shard_map/ppermute | solution.py:430
  8.9 0.0 copy-done
  8.9 0.0 collective-permute-start.7
  8.9 2.2 %collective-permute-start.2 = (bf16[64,1024]{1,0:T(8,128)(2,1)S(1)}, bf16[64,1024]{1,0:T(8,128)(2,1)S(1)}, u32[]{:S(2)}, u32[]{:S(2)}) collective-permute-start(bf16[64,1024]{1,0:T(8,128)(2,1)S(1)} %get-tuple-element.21), channel_id=1, source_target_pairs={{0,24},{4,28},{8,0},{12,4},{16,8},{20,12},{24,16},{28,20},{1,25},{... | collective-permute-start | bytes 393224 | tf_op jit(solution)/shard_map/ppermute | solution.py:430
  11.1 1.2 %collective-permute-start.3 = (bf16[64,1024]{1,0:T(8,128)(2,1)S(1)}, bf16[64,1024]{1,0:T(8,128)(2,1)S(1)}, u32[]{:S(2)}, u32[]{:S(2)}) collective-permute-start(bf16[64,1024]{1,0:T(8,128)(2,1)S(1)} %get-tuple-element.22), channel_id=1, source_target_pairs={{0,20},{4,16},{8,28},{12,24},{16,4},{20,0},{24,12},{28,8},{1,21},{... | collective-permute-start | bytes 393224 | tf_op jit(solution)/shard_map/ppermute | solution.py:430
  12.3 1.3 %collective-permute-done.7.refs_9_ = f32[32,128]{1,0:T(8,128)S(1)} collective-permute-done((f32[32,128]{1,0:T(8,128)S(1)}, f32[32,128]{1,0:T(8,128)S(1)}, u32[]{:S(2)}, u32[]{:S(2)}) %collective-permute-start.7) | collective-permute-done | bytes 16416 | tf_op jit(solution)/shard_map/ppermute | solution.py:126
  13.6 1.7 %collective-permute-start.4 = (bf16[64,1024]{1,0:T(8,128)(2,1)S(1)}, bf16[64,1024]{1,0:T(8,128)(2,1)S(1)}, u32[]{:S(2)}, u32[]{:S(2)}) collective-permute-start(bf16[64,1024]{1,0:T(8,128)(2,1)S(1)} %get-tuple-element.23), channel_id=1, source_target_pairs={{0,8},{4,12},{8,16},{12,20},{16,24},{20,28},{24,0},{28,4},{1,9},{5... | collective-permute-start | bytes 393224 | tf_op jit(solution)/shard_map/ppermute | solution.py:430
  15.4 0.0 collective-permute-done.refs_1_
  15.4 3.4 %collective-permute-start.5 = (bf16[64,1024]{1,0:T(8,128)(2,1)S(1)}, bf16[64,1024]{1,0:T(8,128)(2,1)S(1)}, u32[]{:S(2)}, u32[]{:S(2)}) collective-permute-start(bf16[64,1024]{1,0:T(8,128)(2,1)S(1)} %get-tuple-element.24), channel_id=1, source_target_pairs={{0,28},{4,24},{8,4},{12,0},{16,12},{20,8},{24,20},{28,16},{1,29},{... | collective-permute-start | bytes 393224 | tf_op jit(solution)/shard_map/ppermute | solution.py:430
  18.7 0.0 collective-permute-done.1.refs_2_
  18.7 2.0 %collective-permute-start.6 = (bf16[64,1024]{1,0:T(8,128)(2,1)S(1)}, bf16[64,1024]{1,0:T(8,128)(2,1)S(1)}, u32[]{:S(2)}, u32[]{:S(2)}) collective-permute-start(bf16[64,1024]{1,0:T(8,128)(2,1)S(1)} %get-tuple-element.25), channel_id=1, source_target_pairs={{0,4},{4,0},{8,12},{12,8},{16,20},{20,16},{24,28},{28,24},{1,5},{5... | collective-permute-start | bytes 393224 | tf_op jit(solution)/shard_map/ppermute | solution.py:430
  20.7 0.0 collective-permute-done.2.refs_3_
  20.7 6.6 %collective-permute-done.3.refs_4_ = bf16[64,1024]{1,0:T(8,128)(2,1)S(1)} collective-permute-done((bf16[64,1024]{1,0:T(8,128)(2,1)S(1)}, bf16[64,1024]{1,0:T(8,128)(2,1)S(1)}, u32[]{:S(2)}, u32[]{:S(2)}) %collective-permute-start.3) | collective-permute-done | bytes 131104 | tf_op jit(solution)/shard_map/ppermute | solution.py:430
  27.3 0.0 collective-permute-done.4.refs_5_
  27.3 0.0 collective-permute-done.5.refs_6_
  27.3 0.0 collective-permute-done.6.refs_7_
  27.3 2.4 %gram.1 = (f32[512,128]{1,0:T(8,128)S(1)}, f32[512,128]{1,0:T(8,128)S(1)}, f32[64,128]{1,0:T(8,128)S(1)}) custom-call(bf16[64,1024]{1,0:T(8,128)(2,1)S(1)} %get-tuple-element.19.refs_0_, bf16[64,1024]{1,0:T(8,128)(2,1)S(1)} %collective-permute-done.refs_1_, bf16[64,1024]{1,0:T(8,128)(2,1)S(1)} %collective-permute-done.1.refs_2_, ...), custom_call_target="tpu_custom_call" | custom-call | tf_op jit(solution)/shard_map/gram/pallas_call | solution.py:438
  29.7 0.1 collective-permute-start.8
  29.8 1.5 %collective-permute-done.8.got_ref = f32[512,128]{1,0:T(8,128)S(1)} collective-permute-done((f32[512,128]{1,0:T(8,128)S(1)}, f32[512,128]{1,0:T(8,128)S(1)}, u32[]{:S(2)}, u32[]{:S(2)}) %collective-permute-start.8) | collective-permute-done | bytes 262176 | tf_op jit(solution)/shard_map/ppermute | solution.py:126
  31.3 1.8 %collective-permute-start.9 = (f32[128,128]{1,0:T(8,128)S(1)}, f32[128,128]{1,0:T(8,128)S(1)}, u32[]{:S(2)}, u32[]{:S(2)}) collective-permute-start(f32[128,128]{1,0:T(8,128)S(1)} %get-tuple-element.29), channel_id=1, source_target_pairs={{0,6},{1,7},{2,4},{3,5},{4,2},{5,3},{6,0},{7,1},{8,14},{9,15},{10,... | collective-permute-start | bytes 196616 | tf_op jit(solution)/shard_map/ppermute | solution.py:136
  33.1 0.4 collective-permute-start.10
  33.5 1.4 %collective-permute-start.11 = (f32[128,128]{1,0:T(8,128)S(1)}, f32[128,128]{1,0:T(8,128)S(1)}, u32[]{:S(2)}, u32[]{:S(2)}) collective-permute-start(f32[128,128]{1,0:T(8,128)S(1)} %get-tuple-element.31), channel_id=1, source_target_pairs={{0,4},{1,5},{2,6},{3,7},{4,0},{5,1},{6,2},{7,3},{8,12},{9,13},{10,... | collective-permute-start | bytes 196616 | tf_op jit(solution)/shard_map/ppermute | solution.py:136
  34.9 1.7 %collective-permute-done.9 = f32[128,128]{1,0:T(8,128)S(1)} collective-permute-done((f32[128,128]{1,0:T(8,128)S(1)}, f32[128,128]{1,0:T(8,128)S(1)}, u32[]{:S(2)}, u32[]{:S(2)}) %collective-permute-start.9) | collective-permute-done | bytes 65568 | tf_op jit(solution)/shard_map/ppermute | solution.py:136
  36.6 1.3 %collective-permute-done.10 = f32[128,128]{1,0:T(8,128)S(1)} collective-permute-done((f32[128,128]{1,0:T(8,128)S(1)}, f32[128,128]{1,0:T(8,128)S(1)}, u32[]{:S(2)}, u32[]{:S(2)}) %collective-permute-start.10) | collective-permute-done | bytes 65568 | tf_op jit(solution)/shard_map/ppermute | solution.py:136
  37.8 0.0 collective-permute-done.11
  37.9 4.3 %collective-permute-start.14 = (f32[128,128]{1,0:T(8,128)S(1)}, f32[128,128]{1,0:T(8,128)S(1)}, u32[]{:S(2)}, u32[]{:S(2)}) collective-permute-start(f32[128,128]{1,0:T(8,128)S(1)} %add_add_fusion.1), channel_id=1, source_target_pairs={{0,16},{8,24},{16,0},{24,8},{1,17},{9,25},{17,1},{25,9},{2,18},{10... | collective-permute-start | bytes 196616 | tf_op jit(solution)/shard_map/ppermute | solution.py:126
  42.2 0.5 collective-permute-start.13
  42.7 0.1 collective-permute-start.12
  42.8 3.9 %collective-permute-done.14 = f32[128,128]{1,0:T(8,128)S(1)} collective-permute-done((f32[128,128]{1,0:T(8,128)S(1)}, f32[128,128]{1,0:T(8,128)S(1)}, u32[]{:S(2)}, u32[]{:S(2)}) %collective-permute-start.14) | collective-permute-done | bytes 65568 | tf_op jit(solution)/shard_map/ppermute | solution.py:126
  46.7 1.6 %collective-permute-done.13 = f32[128,128]{1,0:T(8,128)S(1)} collective-permute-done((f32[128,128]{1,0:T(8,128)S(1)}, f32[128,128]{1,0:T(8,128)S(1)}, u32[]{:S(2)}, u32[]{:S(2)}) %collective-permute-start.13) | collective-permute-done | bytes 65568 | tf_op jit(solution)/shard_map/ppermute | solution.py:126
  48.3 0.0 collective-permute-done.12
  48.3 1.7 %collective-permute-start.17 = (f32[128,128]{1,0:T(8,128)S(1)}, f32[128,128]{1,0:T(8,128)S(1)}, u32[]{:S(2)}, u32[]{:S(2)}) collective-permute-start(f32[128,128]{1,0:T(8,128)S(1)} %add_add_fusion.refs_0_), channel_id=1, source_target_pairs={{0,6},{1,7},{2,4},{3,5},{4,2},{5,3},{6,0},{7,1},{8,14},{9,15},{10,... | collective-permute-start | bytes 196616 | tf_op jit(solution)/shard_map/ppermute | solution.py:136
  50.0 1.3 %collective-permute-start.16 = (f32[128,128]{1,0:T(8,128)S(1)}, f32[128,128]{1,0:T(8,128)S(1)}, u32[]{:S(2)}, u32[]{:S(2)}) collective-permute-start(f32[128,128]{1,0:T(8,128)S(1)} %add_add_fusion.refs_0_), channel_id=1, source_target_pairs={{0,4},{1,5},{2,6},{3,7},{4,0},{5,1},{6,2},{7,3},{8,12},{9,13},{10,... | collective-permute-start | bytes 196616 | tf_op jit(solution)/shard_map/ppermute | solution.py:136
  51.3 0.5 collective-permute-start.15
  51.8 0.0 collective-permute-start.18
  51.8 1.7 %collective-permute-done.17.refs_3_ = f32[128,128]{1,0:T(8,128)S(1)} collective-permute-done((f32[128,128]{1,0:T(8,128)S(1)}, f32[128,128]{1,0:T(8,128)S(1)}, u32[]{:S(2)}, u32[]{:S(2)}) %collective-permute-start.17) | collective-permute-done | bytes 65568 | tf_op jit(solution)/shard_map/ppermute | solution.py:136
  53.5 0.0 collective-permute-start.21
  53.5 0.8 %collective-permute-done.16.refs_2_ = f32[128,128]{1,0:T(8,128)S(1)} collective-permute-done((f32[128,128]{1,0:T(8,128)S(1)}, f32[128,128]{1,0:T(8,128)S(1)}, u32[]{:S(2)}, u32[]{:S(2)}) %collective-permute-start.16) | collective-permute-done | bytes 65568 | tf_op jit(solution)/shard_map/ppermute | solution.py:136
  54.3 0.0 collective-permute-start.20
  54.3 1.3 %collective-permute-done.15.refs_1_ = f32[128,128]{1,0:T(8,128)S(1)} collective-permute-done((f32[128,128]{1,0:T(8,128)S(1)}, f32[128,128]{1,0:T(8,128)S(1)}, u32[]{:S(2)}, u32[]{:S(2)}) %collective-permute-start.15) | collective-permute-done | bytes 65568 | tf_op jit(solution)/shard_map/ppermute | solution.py:136
  55.6 0.0 collective-permute-start.19
  55.6 1.3 %collective-permute-start.22 = (f32[64,128]{1,0:T(8,128)S(1)}, f32[64,128]{1,0:T(8,128)S(1)}, u32[]{:S(2)}, u32[]{:S(2)}) collective-permute-start(f32[64,128]{1,0:T(8,128)S(1)} %get-tuple-element.32.refs_8_), channel_id=1, source_target_pairs={{0,16},{8,24},{16,0},{24,8},{1,17},{9,25},{17,1},{25,9},{2,18},{10... | collective-permute-start | bytes 98312 | tf_op jit(solution)/shard_map/ppermute | solution.py:126
  56.9 3.7 %collective-permute-done.22.refs_9_ = f32[64,128]{1,0:T(8,128)S(1)} collective-permute-done((f32[64,128]{1,0:T(8,128)S(1)}, f32[64,128]{1,0:T(8,128)S(1)}, u32[]{:S(2)}, u32[]{:S(2)}) %collective-permute-start.22) | collective-permute-done | bytes 32800 | tf_op jit(solution)/shard_map/ppermute | solution.py:126
  60.5 0.0 collective-permute-done.18.refs_4_
  60.5 0.0 collective-permute-done.21.refs_7_
  60.5 0.0 collective-permute-done.20.refs_6_
  60.5 0.0 collective-permute-done.19.refs_5_
  60.5 5.2 %finish.1 = f32[32,128]{1,0:T(8,128)} custom-call(f32[128,128]{1,0:T(8,128)S(1)} %add_add_fusion.refs_0_, f32[128,128]{1,0:T(8,128)S(1)} %collective-permute-done.15.refs_1_, f32[128,128]{1,0:T(8,128)S(1)} %collective-permute-done.16.refs_2_, f32[128,128]{1,0:T(8,128)S(1)} %collective-permute-done.17.refs_3_, ...), custom_call_target="tpu_custom_call" | custom-call | tf_op jit(solution)/shard_map/finish/pallas_call | solution.py:464
  (3 shorter events, 0.1 us)
Async XLA Ops:
  0.8 8.0 %copy-start = (f32[128,32]{0,1:T(8,128)S(1)}, f32[128,32]{0,1:T(8,128)}, u32[]{:S(2)}) copy-start(f32[128,32]{0,1:T(8,128)} %param.3) | copy-start | bytes 49156
  0.9 14.5 %collective-permute-start = (bf16[64,1024]{1,0:T(8,128)(2,1)S(1)}, bf16[64,1024]{1,0:T(8,128)(2,1)S(1)}, u32[]{:S(2)}, u32[]{:S(2)}) collective-permute-start(bf16[64,1024]{1,0:T(8,128)(2,1)S(1)} %cut.3), channel_id=1, source_target_pairs={{0,16},{4,20},{8,24},{12,28},{16,0},{20,4},{24,8},{28,12},{1,17},{... | collective-permute-start | bytes 393224 | tf_op jit(solution)/shard_map/ppermute | solution.py:430
  6.3 12.4 %collective-permute-start.1 = (bf16[64,1024]{1,0:T(8,128)(2,1)S(1)}, bf16[64,1024]{1,0:T(8,128)(2,1)S(1)}, u32[]{:S(2)}, u32[]{:S(2)}) collective-permute-start(bf16[64,1024]{1,0:T(8,128)(2,1)S(1)} %get-tuple-element.20), channel_id=1, source_target_pairs={{0,12},{4,8},{8,20},{12,16},{16,28},{20,24},{24,4},{28,0},{1,13},{... | collective-permute-start | bytes 393224 | tf_op jit(solution)/shard_map/ppermute | solution.py:430
  8.9 4.8 %collective-permute-start.7 = (f32[32,128]{1,0:T(8,128)S(1)}, f32[32,128]{1,0:T(8,128)S(1)}, u32[]{:S(2)}, u32[]{:S(2)}) collective-permute-start(f32[32,128]{1,0:T(8,128)S(1)} %bitcast.2), channel_id=1, source_target_pairs={{0,8},{8,0},{16,24},{24,16},{1,9},{9,1},{17,25},{25,17},{2,10},{10... | collective-permute-start | bytes 49160 | tf_op jit(solution)/shard_map/ppermute | solution.py:126
  8.9 11.8 %collective-permute-start.2 = (bf16[64,1024]{1,0:T(8,128)(2,1)S(1)}, bf16[64,1024]{1,0:T(8,128)(2,1)S(1)}, u32[]{:S(2)}, u32[]{:S(2)}) collective-permute-start(bf16[64,1024]{1,0:T(8,128)(2,1)S(1)} %get-tuple-element.21), channel_id=1, source_target_pairs={{0,24},{4,28},{8,0},{12,4},{16,8},{20,12},{24,16},{28,20},{1,25},{... | collective-permute-start | bytes 393224 | tf_op jit(solution)/shard_map/ppermute | solution.py:430
  11.1 16.2 %collective-permute-start.3 = (bf16[64,1024]{1,0:T(8,128)(2,1)S(1)}, bf16[64,1024]{1,0:T(8,128)(2,1)S(1)}, u32[]{:S(2)}, u32[]{:S(2)}) collective-permute-start(bf16[64,1024]{1,0:T(8,128)(2,1)S(1)} %get-tuple-element.22), channel_id=1, source_target_pairs={{0,20},{4,16},{8,28},{12,24},{16,4},{20,0},{24,12},{28,8},{1,21},{... | collective-permute-start | bytes 393224 | tf_op jit(solution)/shard_map/ppermute | solution.py:430
  13.6 13.7 %collective-permute-start.4 = (bf16[64,1024]{1,0:T(8,128)(2,1)S(1)}, bf16[64,1024]{1,0:T(8,128)(2,1)S(1)}, u32[]{:S(2)}, u32[]{:S(2)}) collective-permute-start(bf16[64,1024]{1,0:T(8,128)(2,1)S(1)} %get-tuple-element.23), channel_id=1, source_target_pairs={{0,8},{4,12},{8,16},{12,20},{16,24},{20,28},{24,0},{28,4},{1,9},{5... | collective-permute-start | bytes 393224 | tf_op jit(solution)/shard_map/ppermute | solution.py:430
  15.4 12.0 %collective-permute-start.5 = (bf16[64,1024]{1,0:T(8,128)(2,1)S(1)}, bf16[64,1024]{1,0:T(8,128)(2,1)S(1)}, u32[]{:S(2)}, u32[]{:S(2)}) collective-permute-start(bf16[64,1024]{1,0:T(8,128)(2,1)S(1)} %get-tuple-element.24), channel_id=1, source_target_pairs={{0,28},{4,24},{8,4},{12,0},{16,12},{20,8},{24,20},{28,16},{1,29},{... | collective-permute-start | bytes 393224 | tf_op jit(solution)/shard_map/ppermute | solution.py:430
  18.7 8.6 %collective-permute-start.6 = (bf16[64,1024]{1,0:T(8,128)(2,1)S(1)}, bf16[64,1024]{1,0:T(8,128)(2,1)S(1)}, u32[]{:S(2)}, u32[]{:S(2)}) collective-permute-start(bf16[64,1024]{1,0:T(8,128)(2,1)S(1)} %get-tuple-element.25), channel_id=1, source_target_pairs={{0,4},{4,0},{8,12},{12,8},{16,20},{20,16},{24,28},{28,24},{1,5},{5... | collective-permute-start | bytes 393224 | tf_op jit(solution)/shard_map/ppermute | solution.py:430
  29.7 1.6 %collective-permute-start.8 = (f32[512,128]{1,0:T(8,128)S(1)}, f32[512,128]{1,0:T(8,128)S(1)}, u32[]{:S(2)}, u32[]{:S(2)}) collective-permute-start(f32[512,128]{1,0:T(8,128)S(1)} %get-tuple-element.27), channel_id=1, source_target_pairs={{0,1},{1,0},{2,3},{3,2},{4,5},{5,4},{6,7},{7,6},{8,9},{9,8},{10,11... | collective-permute-start | bytes 786440 | tf_op jit(solution)/shard_map/ppermute | solution.py:126
  31.3 5.2 %collective-permute-start.9 = (f32[128,128]{1,0:T(8,128)S(1)}, f32[128,128]{1,0:T(8,128)S(1)}, u32[]{:S(2)}, u32[]{:S(2)}) collective-permute-start(f32[128,128]{1,0:T(8,128)S(1)} %get-tuple-element.29), channel_id=1, source_target_pairs={{0,6},{1,7},{2,4},{3,5},{4,2},{5,3},{6,0},{7,1},{8,14},{9,15},{10,... | collective-permute-start | bytes 196616 | tf_op jit(solution)/shard_map/ppermute | solution.py:136
  33.1 4.7 %collective-permute-start.10 = (f32[128,128]{1,0:T(8,128)S(1)}, f32[128,128]{1,0:T(8,128)S(1)}, u32[]{:S(2)}, u32[]{:S(2)}) collective-permute-start(f32[128,128]{1,0:T(8,128)S(1)} %get-tuple-element.30), channel_id=1, source_target_pairs={{0,2},{1,3},{2,0},{3,1},{4,6},{5,7},{6,4},{7,5},{8,10},{9,11},{10,... | collective-permute-start | bytes 196616 | tf_op jit(solution)/shard_map/ppermute | solution.py:136
  33.5 4.4 %collective-permute-start.11 = (f32[128,128]{1,0:T(8,128)S(1)}, f32[128,128]{1,0:T(8,128)S(1)}, u32[]{:S(2)}, u32[]{:S(2)}) collective-permute-start(f32[128,128]{1,0:T(8,128)S(1)} %get-tuple-element.31), channel_id=1, source_target_pairs={{0,4},{1,5},{2,6},{3,7},{4,0},{5,1},{6,2},{7,3},{8,12},{9,13},{10,... | collective-permute-start | bytes 196616 | tf_op jit(solution)/shard_map/ppermute | solution.py:136
  37.9 8.8 %collective-permute-start.14 = (f32[128,128]{1,0:T(8,128)S(1)}, f32[128,128]{1,0:T(8,128)S(1)}, u32[]{:S(2)}, u32[]{:S(2)}) collective-permute-start(f32[128,128]{1,0:T(8,128)S(1)} %add_add_fusion.1), channel_id=1, source_target_pairs={{0,16},{8,24},{16,0},{24,8},{1,17},{9,25},{17,1},{25,9},{2,18},{10... | collective-permute-start | bytes 196616 | tf_op jit(solution)/shard_map/ppermute | solution.py:126
  42.2 6.1 %collective-permute-start.13 = (f32[128,128]{1,0:T(8,128)S(1)}, f32[128,128]{1,0:T(8,128)S(1)}, u32[]{:S(2)}, u32[]{:S(2)}) collective-permute-start(f32[128,128]{1,0:T(8,128)S(1)} %add_add_fusion.1), channel_id=1, source_target_pairs={{0,24},{8,16},{16,8},{24,0},{1,25},{9,17},{17,9},{25,1},{2,26},{10... | collective-permute-start | bytes 196616 | tf_op jit(solution)/shard_map/ppermute | solution.py:126
  42.7 5.5 %collective-permute-start.12 = (f32[128,128]{1,0:T(8,128)S(1)}, f32[128,128]{1,0:T(8,128)S(1)}, u32[]{:S(2)}, u32[]{:S(2)}) collective-permute-start(f32[128,128]{1,0:T(8,128)S(1)} %add_add_fusion.1), channel_id=1, source_target_pairs={{0,8},{8,0},{16,24},{24,16},{1,9},{9,1},{17,25},{25,17},{2,10},{10... | collective-permute-start | bytes 196616 | tf_op jit(solution)/shard_map/ppermute | solution.py:126
  48.3 5.2 %collective-permute-start.17 = (f32[128,128]{1,0:T(8,128)S(1)}, f32[128,128]{1,0:T(8,128)S(1)}, u32[]{:S(2)}, u32[]{:S(2)}) collective-permute-start(f32[128,128]{1,0:T(8,128)S(1)} %add_add_fusion.refs_0_), channel_id=1, source_target_pairs={{0,6},{1,7},{2,4},{3,5},{4,2},{5,3},{6,0},{7,1},{8,14},{9,15},{10,... | collective-permute-start | bytes 196616 | tf_op jit(solution)/shard_map/ppermute | solution.py:136
  50.0 4.3 %collective-permute-start.16 = (f32[128,128]{1,0:T(8,128)S(1)}, f32[128,128]{1,0:T(8,128)S(1)}, u32[]{:S(2)}, u32[]{:S(2)}) collective-permute-start(f32[128,128]{1,0:T(8,128)S(1)} %add_add_fusion.refs_0_), channel_id=1, source_target_pairs={{0,4},{1,5},{2,6},{3,7},{4,0},{5,1},{6,2},{7,3},{8,12},{9,13},{10,... | collective-permute-start | bytes 196616 | tf_op jit(solution)/shard_map/ppermute | solution.py:136
  51.3 4.3 %collective-permute-start.15 = (f32[128,128]{1,0:T(8,128)S(1)}, f32[128,128]{1,0:T(8,128)S(1)}, u32[]{:S(2)}, u32[]{:S(2)}) collective-permute-start(f32[128,128]{1,0:T(8,128)S(1)} %add_add_fusion.refs_0_), channel_id=1, source_target_pairs={{0,2},{1,3},{2,0},{3,1},{4,6},{5,7},{6,4},{7,5},{8,10},{9,11},{10,... | collective-permute-start | bytes 196616 | tf_op jit(solution)/shard_map/ppermute | solution.py:136
  51.8 8.7 %collective-permute-start.18 = (f32[128,128]{1,0:T(8,128)S(1)}, f32[128,128]{1,0:T(8,128)S(1)}, u32[]{:S(2)}, u32[]{:S(2)}) collective-permute-start(f32[128,128]{1,0:T(8,128)S(1)} %add_add_fusion.refs_0_), channel_id=1, source_target_pairs={{0,1},{1,0},{2,3},{3,2},{4,5},{5,4},{6,7},{7,6},{8,9},{9,8},{10,11... | collective-permute-start | bytes 196616 | tf_op jit(solution)/shard_map/ppermute | solution.py:126
  53.5 7.0 %collective-permute-start.21 = (f32[128,128]{1,0:T(8,128)S(1)}, f32[128,128]{1,0:T(8,128)S(1)}, u32[]{:S(2)}, u32[]{:S(2)}) collective-permute-start(f32[128,128]{1,0:T(8,128)S(1)} %collective-permute-done.17.refs_3_), channel_id=1, source_target_pairs={{0,1},{1,0},{2,3},{3,2},{4,5},{5,4},{6,7},{7,6},{8,9},{9,8},{10,11... | collective-permute-start | bytes 196616 | tf_op jit(solution)/shard_map/ppermute | solution.py:126
  54.3 6.3 %collective-permute-start.20 = (f32[128,128]{1,0:T(8,128)S(1)}, f32[128,128]{1,0:T(8,128)S(1)}, u32[]{:S(2)}, u32[]{:S(2)}) collective-permute-start(f32[128,128]{1,0:T(8,128)S(1)} %collective-permute-done.16.refs_2_), channel_id=1, source_target_pairs={{0,1},{1,0},{2,3},{3,2},{4,5},{5,4},{6,7},{7,6},{8,9},{9,8},{10,11... | collective-permute-start | bytes 196616 | tf_op jit(solution)/shard_map/ppermute | solution.py:126
  55.6 4.9 %collective-permute-start.19 = (f32[128,128]{1,0:T(8,128)S(1)}, f32[128,128]{1,0:T(8,128)S(1)}, u32[]{:S(2)}, u32[]{:S(2)}) collective-permute-start(f32[128,128]{1,0:T(8,128)S(1)} %collective-permute-done.15.refs_1_), channel_id=1, source_target_pairs={{0,1},{1,0},{2,3},{3,2},{4,5},{5,4},{6,7},{7,6},{8,9},{9,8},{10,11... | collective-permute-start | bytes 196616 | tf_op jit(solution)/shard_map/ppermute | solution.py:126
  55.6 4.9 %collective-permute-start.22 = (f32[64,128]{1,0:T(8,128)S(1)}, f32[64,128]{1,0:T(8,128)S(1)}, u32[]{:S(2)}, u32[]{:S(2)}) collective-permute-start(f32[64,128]{1,0:T(8,128)S(1)} %get-tuple-element.32.refs_8_), channel_id=1, source_target_pairs={{0,16},{8,24},{16,0},{24,8},{1,17},{9,25},{17,1},{25,9},{2,18},{10... | collective-permute-start | bytes 98312 | tf_op jit(solution)/shard_map/ppermute | solution.py:126
where the time goes:
time: 66 us; the launch traced here: 65.8 us
  starting transfers between devices  30.6 us (46%)
  waiting for transfers between devices  25.3 us (38%)
  Pallas kernels  9.77 us (15%)
    ppermute x7, starting transfers between devices, packed_plan(): received.append(lax.ppermute(cuts[step], ('row', 'col'), pairs))  17.2 us
    ppermute x10, waiting for transfers between devices, xor_permute(): lax.ppermute(x, axis, [(i, i ^ mask) for i in range(lax.axis_size(axis))])  11.9 us
    ppermute x6, starting transfers between devices, quad_permute(): return lax.ppermute(x, ('col', 'feat'), pairs)  7.11 us
    ppermute x6, waiting for transfers between devices, quad_permute(): return lax.ppermute(x, ('col', 'feat'), pairs)  6.74 us
    ppermute x7, waiting for transfers between devices, packed_plan(): received.append(lax.ppermute(cuts[step], ('row', 'col'), pairs))  6.65 us
    ppermute x10, starting transfers between devices, xor_permute(): lax.ppermute(x, axis, [(i, i ^ mask) for i in range(lax.axis_size(axis))])  6.28 us
    pallas_call x1, Pallas kernels, packed_plan(): pl.pallas_call(functools.partial(finish_kernel, float(points), tiles, chu...  5.24 us
    pallas_call x1, Pallas kernels, packed_plan(): pl.pallas_call(functools.partial(gram_kernel, steps, rows_total, cols, sh...  2.36 us
  transfers between devices with their start and end apart: 23, of which 11 were waited for; matrix products, arithmetic and copies ran while one was open for 0% of the time, Pallas kernels for 2%

commit v1 on v0

--- a/solution.py
+++ b/solution.py
@@ -339,10 +339,13 @@
             counts = jnp.minimum(block * TILE + jnp.minimum(sub, lane), LAGS - 1) + 1
             lagged = jnp.where(lane == sub, 0.0, lagged)
             keep(jnp.exp(lagged * factor(counts)), block, block)
-    ones = jnp.ones((16, snaps), bf16)
-    degrees = jnp.dot(ones, high_ref[...], preferred_element_type=f32)
-    degrees = degrees + jnp.dot(ones, low_ref[...], preferred_element_type=f32)
-    inverse = 1.0 / degrees[0:1, :]
+    rows_sum = jnp.zeros((8, snaps), f32)
+    for block in range(0, snaps, 64):
+        both = slice(block, block + 64)
+        part = high_ref[both, :].astype(f32) + low_ref[both, :].astype(f32)
+        for at in range(0, 64, 8):
+            rows_sum = rows_sum + part[at : at + 8, :]
+    inverse = 1.0 / jnp.sum(rows_sum, axis=0, keepdims=True)
     scales = lax.sqrt(inverse)
     vecs = begins[0].shape[0] // 2
     for mask in range(4):

time: 66 us -> 66 us (level)
  no operation moved by 1% of the time
where the time goes in v1:
time: 66 us; the launch traced here: 65.8 us
  starting transfers between devices  30.6 us (46%)
  waiting for transfers between devices  25.3 us (38%)
  Pallas kernels  9.76 us (15%)
    ppermute x7, starting transfers between devices, packed_plan(): received.append(lax.ppermute(cuts[step], ('row', 'col'), pairs))  17.2 us
    ppermute x10, waiting for transfers between devices, xor_permute(): lax.ppermute(x, axis, [(i, i ^ mask) for i in range(lax.axis_size(axis))])  11.9 us
    ppermute x6, starting transfers between devices, quad_permute(): return lax.ppermute(x, ('col', 'feat'), pairs)  7.11 us
    ppermute x6, waiting for transfers between devices, quad_permute(): return lax.ppermute(x, ('col', 'feat'), pairs)  6.74 us
    ppermute x7, waiting for transfers between devices, packed_plan(): received.append(lax.ppermute(cuts[step], ('row', 'col'), pairs))  6.65 us
    ppermute x10, starting transfers between devices, xor_permute(): lax.ppermute(x, axis, [(i, i ^ mask) for i in range(lax.axis_size(axis))])  6.28 us
    pallas_call x1, Pallas kernels, packed_plan(): pl.pallas_call(functools.partial(finish_kernel, float(points), tiles, chu...  5.23 us
    pallas_call x1, Pallas kernels, packed_plan(): pl.pallas_call(functools.partial(gram_kernel, steps, rows_total, cols, sh...  2.36 us
  transfers between devices with their start and end apart: 23, of which 11 were waited for; matrix products, arithmetic and copies ran while one was open for 0% of the time, Pallas kernels for 2%

profile of v1, /device:TPU:0, one launch (start us, length us, event | category | flops | bytes accessed | tf_op | source)
XLA Modules:
  0.0 65.8 jit_solution(7199091755731986490)
XLA Ops:
  0.0 0.8 %cut.3 = bf16[64,1024]{1,0:T(8,128)(2,1)S(1)} custom-call(bf16[64,8192]{1,0:T(8,128)(2,1)} %x_ref.3), custom_call_target="tpu_custom_call" | custom-call | tf_op jit(solution)/shard_map/cut/pallas_call | solution.py:416
  0.8 0.0 copy-start
  0.9 4.1 %collective-permute-start = (bf16[64,1024]{1,0:T(8,128)(2,1)S(1)}, bf16[64,1024]{1,0:T(8,128)(2,1)S(1)}, u32[]{:S(2)}, u32[]{:S(2)}) collective-permute-start(bf16[64,1024]{1,0:T(8,128)(2,1)S(1)} %cut.3), channel_id=1, source_target_pairs={{0,16},{4,20},{8,24},{12,28},{16,0},{20,4},{24,8},{28,12},{1,17},{... | collective-permute-start | bytes 393224 | tf_op jit(solution)/shard_map/ppermute | solution.py:433
  5.0 1.3 %cut.2 = (bf16[64,1024]{1,0:T(8,128)(2,1)S(1)}, bf16[64,1024]{1,0:T(8,128)(2,1)S(1)}, bf16[64,1024]{1,0:T(8,128)(2,1)S(1)}, bf16[64,1024]{1,0:T(8,128)(2,1)S(1)}...) custom-call(bf16[64,8192]{1,0:T(8,128)(2,1)} %x_ref.3), custom_call_target="tpu_custom_call" | custom-call | tf_op jit(solution)/shard_map/cut/pallas_call | solution.py:416
  6.3 2.6 %collective-permute-start.1 = (bf16[64,1024]{1,0:T(8,128)(2,1)S(1)}, bf16[64,1024]{1,0:T(8,128)(2,1)S(1)}, u32[]{:S(2)}, u32[]{:S(2)}) collective-permute-start(bf16[64,1024]{1,0:T(8,128)(2,1)S(1)} %get-tuple-element.20), channel_id=1, source_target_pairs={{0,12},{4,8},{8,20},{12,16},{16,28},{20,24},{24,4},{28,0},{1,13},{... | collective-permute-start | bytes 393224 | tf_op jit(solution)/shard_map/ppermute | solution.py:433
  8.9 0.0 copy-done
  8.9 0.0 collective-permute-start.7
  8.9 2.2 %collective-permute-start.2 = (bf16[64,1024]{1,0:T(8,128)(2,1)S(1)}, bf16[64,1024]{1,0:T(8,128)(2,1)S(1)}, u32[]{:S(2)}, u32[]{:S(2)}) collective-permute-start(bf16[64,1024]{1,0:T(8,128)(2,1)S(1)} %get-tuple-element.21), channel_id=1, source_target_pairs={{0,24},{4,28},{8,0},{12,4},{16,8},{20,12},{24,16},{28,20},{1,25},{... | collective-permute-start | bytes 393224 | tf_op jit(solution)/shard_map/ppermute | solution.py:433
  11.1 1.2 %collective-permute-start.3 = (bf16[64,1024]{1,0:T(8,128)(2,1)S(1)}, bf16[64,1024]{1,0:T(8,128)(2,1)S(1)}, u32[]{:S(2)}, u32[]{:S(2)}) collective-permute-start(bf16[64,1024]{1,0:T(8,128)(2,1)S(1)} %get-tuple-element.22), channel_id=1, source_target_pairs={{0,20},{4,16},{8,28},{12,24},{16,4},{20,0},{24,12},{28,8},{1,21},{... | collective-permute-start | bytes 393224 | tf_op jit(solution)/shard_map/ppermute | solution.py:433
  12.3 1.3 %collective-permute-done.7.refs_9_ = f32[32,128]{1,0:T(8,128)S(1)} collective-permute-done((f32[32,128]{1,0:T(8,128)S(1)}, f32[32,128]{1,0:T(8,128)S(1)}, u32[]{:S(2)}, u32[]{:S(2)}) %collective-permute-start.7) | collective-permute-done | bytes 16416 | tf_op jit(solution)/shard_map/ppermute | solution.py:126
  13.6 1.7 %collective-permute-start.4 = (bf16[64,1024]{1,0:T(8,128)(2,1)S(1)}, bf16[64,1024]{1,0:T(8,128)(2,1)S(1)}, u32[]{:S(2)}, u32[]{:S(2)}) collective-permute-start(bf16[64,1024]{1,0:T(8,128)(2,1)S(1)} %get-tuple-element.23), channel_id=1, source_target_pairs={{0,8},{4,12},{8,16},{12,20},{16,24},{20,28},{24,0},{28,4},{1,9},{5... | collective-permute-start | bytes 393224 | tf_op jit(solution)/shard_map/ppermute | solution.py:433
  15.4 0.0 collective-permute-done.refs_1_
  15.4 3.4 %collective-permute-start.5 = (bf16[64,1024]{1,0:T(8,128)(2,1)S(1)}, bf16[64,1024]{1,0:T(8,128)(2,1)S(1)}, u32[]{:S(2)}, u32[]{:S(2)}) collective-permute-start(bf16[64,1024]{1,0:T(8,128)(2,1)S(1)} %get-tuple-element.24), channel_id=1, source_target_pairs={{0,28},{4,24},{8,4},{12,0},{16,12},{20,8},{24,20},{28,16},{1,29},{... | collective-permute-start | bytes 393224 | tf_op jit(solution)/shard_map/ppermute | solution.py:433
  18.7 0.0 collective-permute-done.1.refs_2_
  18.7 2.0 %collective-permute-start.6 = (bf16[64,1024]{1,0:T(8,128)(2,1)S(1)}, bf16[64,1024]{1,0:T(8,128)(2,1)S(1)}, u32[]{:S(2)}, u32[]{:S(2)}) collective-permute-start(bf16[64,1024]{1,0:T(8,128)(2,1)S(1)} %get-tuple-element.25), channel_id=1, source_target_pairs={{0,4},{4,0},{8,12},{12,8},{16,20},{20,16},{24,28},{28,24},{1,5},{5... | collective-permute-start | bytes 393224 | tf_op jit(solution)/shard_map/ppermute | solution.py:433
  20.7 0.0 collective-permute-done.2.refs_3_
  20.7 6.6 %collective-permute-done.3.refs_4_ = bf16[64,1024]{1,0:T(8,128)(2,1)S(1)} collective-permute-done((bf16[64,1024]{1,0:T(8,128)(2,1)S(1)}, bf16[64,1024]{1,0:T(8,128)(2,1)S(1)}, u32[]{:S(2)}, u32[]{:S(2)}) %collective-permute-start.3) | collective-permute-done | bytes 131104 | tf_op jit(solution)/shard_map/ppermute | solution.py:433
  27.3 0.0 collective-permute-done.4.refs_5_
  27.3 0.0 collective-permute-done.5.refs_6_
  27.3 0.0 collective-permute-done.6.refs_7_
  27.3 2.4 %gram.1 = (f32[512,128]{1,0:T(8,128)S(1)}, f32[512,128]{1,0:T(8,128)S(1)}, f32[64,128]{1,0:T(8,128)S(1)}) custom-call(bf16[64,1024]{1,0:T(8,128)(2,1)S(1)} %get-tuple-element.19.refs_0_, bf16[64,1024]{1,0:T(8,128)(2,1)S(1)} %collective-permute-done.refs_1_, bf16[64,1024]{1,0:T(8,128)(2,1)S(1)} %collective-permute-done.1.refs_2_, ...), custom_call_target="tpu_custom_call" | custom-call | tf_op jit(solution)/shard_map/gram/pallas_call | solution.py:441
  29.7 0.1 collective-permute-start.8
  29.8 1.5 %collective-permute-done.8.got_ref = f32[512,128]{1,0:T(8,128)S(1)} collective-permute-done((f32[512,128]{1,0:T(8,128)S(1)}, f32[512,128]{1,0:T(8,128)S(1)}, u32[]{:S(2)}, u32[]{:S(2)}) %collective-permute-start.8) | collective-permute-done | bytes 262176 | tf_op jit(solution)/shard_map/ppermute | solution.py:126
  31.3 1.8 %collective-permute-start.9 = (f32[128,128]{1,0:T(8,128)S(1)}, f32[128,128]{1,0:T(8,128)S(1)}, u32[]{:S(2)}, u32[]{:S(2)}) collective-permute-start(f32[128,128]{1,0:T(8,128)S(1)} %get-tuple-element.29), channel_id=1, source_target_pairs={{0,6},{1,7},{2,4},{3,5},{4,2},{5,3},{6,0},{7,1},{8,14},{9,15},{10,... | collective-permute-start | bytes 196616 | tf_op jit(solution)/shard_map/ppermute | solution.py:136
  33.1 0.4 collective-permute-start.10
  33.5 1.4 %collective-permute-start.11 = (f32[128,128]{1,0:T(8,128)S(1)}, f32[128,128]{1,0:T(8,128)S(1)}, u32[]{:S(2)}, u32[]{:S(2)}) collective-permute-start(f32[128,128]{1,0:T(8,128)S(1)} %get-tuple-element.31), channel_id=1, source_target_pairs={{0,4},{1,5},{2,6},{3,7},{4,0},{5,1},{6,2},{7,3},{8,12},{9,13},{10,... | collective-permute-start | bytes 196616 | tf_op jit(solution)/shard_map/ppermute | solution.py:136
  34.9 1.7 %collective-permute-done.9 = f32[128,128]{1,0:T(8,128)S(1)} collective-permute-done((f32[128,128]{1,0:T(8,128)S(1)}, f32[128,128]{1,0:T(8,128)S(1)}, u32[]{:S(2)}, u32[]{:S(2)}) %collective-permute-start.9) | collective-permute-done | bytes 65568 | tf_op jit(solution)/shard_map/ppermute | solution.py:136
  36.6 1.3 %collective-permute-done.10 = f32[128,128]{1,0:T(8,128)S(1)} collective-permute-done((f32[128,128]{1,0:T(8,128)S(1)}, f32[128,128]{1,0:T(8,128)S(1)}, u32[]{:S(2)}, u32[]{:S(2)}) %collective-permute-start.10) | collective-permute-done | bytes 65568 | tf_op jit(solution)/shard_map/ppermute | solution.py:136
  37.8 0.0 collective-permute-done.11
  37.9 4.3 %collective-permute-start.14 = (f32[128,128]{1,0:T(8,128)S(1)}, f32[128,128]{1,0:T(8,128)S(1)}, u32[]{:S(2)}, u32[]{:S(2)}) collective-permute-start(f32[128,128]{1,0:T(8,128)S(1)} %add_add_fusion.1), channel_id=1, source_target_pairs={{0,16},{8,24},{16,0},{24,8},{1,17},{9,25},{17,1},{25,9},{2,18},{10... | collective-permute-start | bytes 196616 | tf_op jit(solution)/shard_map/ppermute | solution.py:126
  42.2 0.5 collective-permute-start.13
  42.7 0.1 collective-permute-start.12
  42.8 3.9 %collective-permute-done.14 = f32[128,128]{1,0:T(8,128)S(1)} collective-permute-done((f32[128,128]{1,0:T(8,128)S(1)}, f32[128,128]{1,0:T(8,128)S(1)}, u32[]{:S(2)}, u32[]{:S(2)}) %collective-permute-start.14) | collective-permute-done | bytes 65568 | tf_op jit(solution)/shard_map/ppermute | solution.py:126
  46.7 1.6 %collective-permute-done.13 = f32[128,128]{1,0:T(8,128)S(1)} collective-permute-done((f32[128,128]{1,0:T(8,128)S(1)}, f32[128,128]{1,0:T(8,128)S(1)}, u32[]{:S(2)}, u32[]{:S(2)}) %collective-permute-start.13) | collective-permute-done | bytes 65568 | tf_op jit(solution)/shard_map/ppermute | solution.py:126
  48.3 0.0 collective-permute-done.12
  48.3 1.7 %collective-permute-start.17 = (f32[128,128]{1,0:T(8,128)S(1)}, f32[128,128]{1,0:T(8,128)S(1)}, u32[]{:S(2)}, u32[]{:S(2)}) collective-permute-start(f32[128,128]{1,0:T(8,128)S(1)} %add_add_fusion.refs_0_), channel_id=1, source_target_pairs={{0,6},{1,7},{2,4},{3,5},{4,2},{5,3},{6,0},{7,1},{8,14},{9,15},{10,... | collective-permute-start | bytes 196616 | tf_op jit(solution)/shard_map/ppermute | solution.py:136
  50.0 1.3 %collective-permute-start.16 = (f32[128,128]{1,0:T(8,128)S(1)}, f32[128,128]{1,0:T(8,128)S(1)}, u32[]{:S(2)}, u32[]{:S(2)}) collective-permute-start(f32[128,128]{1,0:T(8,128)S(1)} %add_add_fusion.refs_0_), channel_id=1, source_target_pairs={{0,4},{1,5},{2,6},{3,7},{4,0},{5,1},{6,2},{7,3},{8,12},{9,13},{10,... | collective-permute-start | bytes 196616 | tf_op jit(solution)/shard_map/ppermute | solution.py:136
  51.3 0.5 collective-permute-start.15
  51.8 0.0 collective-permute-start.18
  51.8 1.7 %collective-permute-done.17.refs_3_ = f32[128,128]{1,0:T(8,128)S(1)} collective-permute-done((f32[128,128]{1,0:T(8,128)S(1)}, f32[128,128]{1,0:T(8,128)S(1)}, u32[]{:S(2)}, u32[]{:S(2)}) %collective-permute-start.17) | collective-permute-done | bytes 65568 | tf_op jit(solution)/shard_map/ppermute | solution.py:136
  53.5 0.0 collective-permute-start.21
  53.5 0.8 %collective-permute-done.16.refs_2_ = f32[128,128]{1,0:T(8,128)S(1)} collective-permute-done((f32[128,128]{1,0:T(8,128)S(1)}, f32[128,128]{1,0:T(8,128)S(1)}, u32[]{:S(2)}, u32[]{:S(2)}) %collective-permute-start.16) | collective-permute-done | bytes 65568 | tf_op jit(solution)/shard_map/ppermute | solution.py:136
  54.3 0.0 collective-permute-start.20
  54.3 1.3 %collective-permute-done.15.refs_1_ = f32[128,128]{1,0:T(8,128)S(1)} collective-permute-done((f32[128,128]{1,0:T(8,128)S(1)}, f32[128,128]{1,0:T(8,128)S(1)}, u32[]{:S(2)}, u32[]{:S(2)}) %collective-permute-start.15) | collective-permute-done | bytes 65568 | tf_op jit(solution)/shard_map/ppermute | solution.py:136
  55.6 0.0 collective-permute-start.19
  55.6 1.3 %collective-permute-start.22 = (f32[64,128]{1,0:T(8,128)S(1)}, f32[64,128]{1,0:T(8,128)S(1)}, u32[]{:S(2)}, u32[]{:S(2)}) collective-permute-start(f32[64,128]{1,0:T(8,128)S(1)} %get-tuple-element.32.refs_8_), channel_id=1, source_target_pairs={{0,16},{8,24},{16,0},{24,8},{1,17},{9,25},{17,1},{25,9},{2,18},{10... | collective-permute-start | bytes 98312 | tf_op jit(solution)/shard_map/ppermute | solution.py:126
  56.9 3.7 %collective-permute-done.22.refs_9_ = f32[64,128]{1,0:T(8,128)S(1)} collective-permute-done((f32[64,128]{1,0:T(8,128)S(1)}, f32[64,128]{1,0:T(8,128)S(1)}, u32[]{:S(2)}, u32[]{:S(2)}) %collective-permute-start.22) | collective-permute-done | bytes 32800 | tf_op jit(solution)/shard_map/ppermute | solution.py:126
  60.5 0.0 collective-permute-done.18.refs_4_
  60.5 0.0 collective-permute-done.21.refs_7_
  60.5 0.0 collective-permute-done.20.refs_6_
  60.5 0.0 collective-permute-done.19.refs_5_
  60.5 5.2 %finish.1 = f32[32,128]{1,0:T(8,128)} custom-call(f32[128,128]{1,0:T(8,128)S(1)} %add_add_fusion.refs_0_, f32[128,128]{1,0:T(8,128)S(1)} %collective-permute-done.15.refs_1_, f32[128,128]{1,0:T(8,128)S(1)} %collective-permute-done.16.refs_2_, f32[128,128]{1,0:T(8,128)S(1)} %collective-permute-done.17.refs_3_, ...), custom_call_target="tpu_custom_call" | custom-call | tf_op jit(solution)/shard_map/finish/pallas_call | solution.py:467
  (3 shorter events, 0.1 us)
Async XLA Ops:
  0.8 8.0 %copy-start = (f32[128,32]{0,1:T(8,128)S(1)}, f32[128,32]{0,1:T(8,128)}, u32[]{:S(2)}) copy-start(f32[128,32]{0,1:T(8,128)} %param.3) | copy-start | bytes 49156
  0.9 14.5 %collective-permute-start = (bf16[64,1024]{1,0:T(8,128)(2,1)S(1)}, bf16[64,1024]{1,0:T(8,128)(2,1)S(1)}, u32[]{:S(2)}, u32[]{:S(2)}) collective-permute-start(bf16[64,1024]{1,0:T(8,128)(2,1)S(1)} %cut.3), channel_id=1, source_target_pairs={{0,16},{4,20},{8,24},{12,28},{16,0},{20,4},{24,8},{28,12},{1,17},{... | collective-permute-start | bytes 393224 | tf_op jit(solution)/shard_map/ppermute | solution.py:433
  6.3 12.4 %collective-permute-start.1 = (bf16[64,1024]{1,0:T(8,128)(2,1)S(1)}, bf16[64,1024]{1,0:T(8,128)(2,1)S(1)}, u32[]{:S(2)}, u32[]{:S(2)}) collective-permute-start(bf16[64,1024]{1,0:T(8,128)(2,1)S(1)} %get-tuple-element.20), channel_id=1, source_target_pairs={{0,12},{4,8},{8,20},{12,16},{16,28},{20,24},{24,4},{28,0},{1,13},{... | collective-permute-start | bytes 393224 | tf_op jit(solution)/shard_map/ppermute | solution.py:433
  8.9 4.8 %collective-permute-start.7 = (f32[32,128]{1,0:T(8,128)S(1)}, f32[32,128]{1,0:T(8,128)S(1)}, u32[]{:S(2)}, u32[]{:S(2)}) collective-permute-start(f32[32,128]{1,0:T(8,128)S(1)} %bitcast.2), channel_id=1, source_target_pairs={{0,8},{8,0},{16,24},{24,16},{1,9},{9,1},{17,25},{25,17},{2,10},{10... | collective-permute-start | bytes 49160 | tf_op jit(solution)/shard_map/ppermute | solution.py:126
  8.9 11.8 %collective-permute-start.2 = (bf16[64,1024]{1,0:T(8,128)(2,1)S(1)}, bf16[64,1024]{1,0:T(8,128)(2,1)S(1)}, u32[]{:S(2)}, u32[]{:S(2)}) collective-permute-start(bf16[64,1024]{1,0:T(8,128)(2,1)S(1)} %get-tuple-element.21), channel_id=1, source_target_pairs={{0,24},{4,28},{8,0},{12,4},{16,8},{20,12},{24,16},{28,20},{1,25},{... | collective-permute-start | bytes 393224 | tf_op jit(solution)/shard_map/ppermute | solution.py:433
  11.1 16.2 %collective-permute-start.3 = (bf16[64,1024]{1,0:T(8,128)(2,1)S(1)}, bf16[64,1024]{1,0:T(8,128)(2,1)S(1)}, u32[]{:S(2)}, u32[]{:S(2)}) collective-permute-start(bf16[64,1024]{1,0:T(8,128)(2,1)S(1)} %get-tuple-element.22), channel_id=1, source_target_pairs={{0,20},{4,16},{8,28},{12,24},{16,4},{20,0},{24,12},{28,8},{1,21},{... | collective-permute-start | bytes 393224 | tf_op jit(solution)/shard_map/ppermute | solution.py:433
  13.6 13.7 %collective-permute-start.4 = (bf16[64,1024]{1,0:T(8,128)(2,1)S(1)}, bf16[64,1024]{1,0:T(8,128)(2,1)S(1)}, u32[]{:S(2)}, u32[]{:S(2)}) collective-permute-start(bf16[64,1024]{1,0:T(8,128)(2,1)S(1)} %get-tuple-element.23), channel_id=1, source_target_pairs={{0,8},{4,12},{8,16},{12,20},{16,24},{20,28},{24,0},{28,4},{1,9},{5... | collective-permute-start | bytes 393224 | tf_op jit(solution)/shard_map/ppermute | solution.py:433
  15.4 12.0 %collective-permute-start.5 = (bf16[64,1024]{1,0:T(8,128)(2,1)S(1)}, bf16[64,1024]{1,0:T(8,128)(2,1)S(1)}, u32[]{:S(2)}, u32[]{:S(2)}) collective-permute-start(bf16[64,1024]{1,0:T(8,128)(2,1)S(1)} %get-tuple-element.24), channel_id=1, source_target_pairs={{0,28},{4,24},{8,4},{12,0},{16,12},{20,8},{24,20},{28,16},{1,29},{... | collective-permute-start | bytes 393224 | tf_op jit(solution)/shard_map/ppermute | solution.py:433
  18.7 8.6 %collective-permute-start.6 = (bf16[64,1024]{1,0:T(8,128)(2,1)S(1)}, bf16[64,1024]{1,0:T(8,128)(2,1)S(1)}, u32[]{:S(2)}, u32[]{:S(2)}) collective-permute-start(bf16[64,1024]{1,0:T(8,128)(2,1)S(1)} %get-tuple-element.25), channel_id=1, source_target_pairs={{0,4},{4,0},{8,12},{12,8},{16,20},{20,16},{24,28},{28,24},{1,5},{5... | collective-permute-start | bytes 393224 | tf_op jit(solution)/shard_map/ppermute | solution.py:433
  29.7 1.6 %collective-permute-start.8 = (f32[512,128]{1,0:T(8,128)S(1)}, f32[512,128]{1,0:T(8,128)S(1)}, u32[]{:S(2)}, u32[]{:S(2)}) collective-permute-start(f32[512,128]{1,0:T(8,128)S(1)} %get-tuple-element.27), channel_id=1, source_target_pairs={{0,1},{1,0},{2,3},{3,2},{4,5},{5,4},{6,7},{7,6},{8,9},{9,8},{10,11... | collective-permute-start | bytes 786440 | tf_op jit(solution)/shard_map/ppermute | solution.py:126
  31.3 5.2 %collective-permute-start.9 = (f32[128,128]{1,0:T(8,128)S(1)}, f32[128,128]{1,0:T(8,128)S(1)}, u32[]{:S(2)}, u32[]{:S(2)}) collective-permute-start(f32[128,128]{1,0:T(8,128)S(1)} %get-tuple-element.29), channel_id=1, source_target_pairs={{0,6},{1,7},{2,4},{3,5},{4,2},{5,3},{6,0},{7,1},{8,14},{9,15},{10,... | collective-permute-start | bytes 196616 | tf_op jit(solution)/shard_map/ppermute | solution.py:136
  33.1 4.7 %collective-permute-start.10 = (f32[128,128]{1,0:T(8,128)S(1)}, f32[128,128]{1,0:T(8,128)S(1)}, u32[]{:S(2)}, u32[]{:S(2)}) collective-permute-start(f32[128,128]{1,0:T(8,128)S(1)} %get-tuple-element.30), channel_id=1, source_target_pairs={{0,2},{1,3},{2,0},{3,1},{4,6},{5,7},{6,4},{7,5},{8,10},{9,11},{10,... | collective-permute-start | bytes 196616 | tf_op jit(solution)/shard_map/ppermute | solution.py:136
  33.5 4.4 %collective-permute-start.11 = (f32[128,128]{1,0:T(8,128)S(1)}, f32[128,128]{1,0:T(8,128)S(1)}, u32[]{:S(2)}, u32[]{:S(2)}) collective-permute-start(f32[128,128]{1,0:T(8,128)S(1)} %get-tuple-element.31), channel_id=1, source_target_pairs={{0,4},{1,5},{2,6},{3,7},{4,0},{5,1},{6,2},{7,3},{8,12},{9,13},{10,... | collective-permute-start | bytes 196616 | tf_op jit(solution)/shard_map/ppermute | solution.py:136
  37.9 8.8 %collective-permute-start.14 = (f32[128,128]{1,0:T(8,128)S(1)}, f32[128,128]{1,0:T(8,128)S(1)}, u32[]{:S(2)}, u32[]{:S(2)}) collective-permute-start(f32[128,128]{1,0:T(8,128)S(1)} %add_add_fusion.1), channel_id=1, source_target_pairs={{0,16},{8,24},{16,0},{24,8},{1,17},{9,25},{17,1},{25,9},{2,18},{10... | collective-permute-start | bytes 196616 | tf_op jit(solution)/shard_map/ppermute | solution.py:126
  42.2 6.1 %collective-permute-start.13 = (f32[128,128]{1,0:T(8,128)S(1)}, f32[128,128]{1,0:T(8,128)S(1)}, u32[]{:S(2)}, u32[]{:S(2)}) collective-permute-start(f32[128,128]{1,0:T(8,128)S(1)} %add_add_fusion.1), channel_id=1, source_target_pairs={{0,24},{8,16},{16,8},{24,0},{1,25},{9,17},{17,9},{25,1},{2,26},{10... | collective-permute-start | bytes 196616 | tf_op jit(solution)/shard_map/ppermute | solution.py:126
  42.7 5.5 %collective-permute-start.12 = (f32[128,128]{1,0:T(8,128)S(1)}, f32[128,128]{1,0:T(8,128)S(1)}, u32[]{:S(2)}, u32[]{:S(2)}) collective-permute-start(f32[128,128]{1,0:T(8,128)S(1)} %add_add_fusion.1), channel_id=1, source_target_pairs={{0,8},{8,0},{16,24},{24,16},{1,9},{9,1},{17,25},{25,17},{2,10},{10... | collective-permute-start | bytes 196616 | tf_op jit(solution)/shard_map/ppermute | solution.py:126
  48.3 5.2 %collective-permute-start.17 = (f32[128,128]{1,0:T(8,128)S(1)}, f32[128,128]{1,0:T(8,128)S(1)}, u32[]{:S(2)}, u32[]{:S(2)}) collective-permute-start(f32[128,128]{1,0:T(8,128)S(1)} %add_add_fusion.refs_0_), channel_id=1, source_target_pairs={{0,6},{1,7},{2,4},{3,5},{4,2},{5,3},{6,0},{7,1},{8,14},{9,15},{10,... | collective-permute-start | bytes 196616 | tf_op jit(solution)/shard_map/ppermute | solution.py:136
  50.0 4.3 %collective-permute-start.16 = (f32[128,128]{1,0:T(8,128)S(1)}, f32[128,128]{1,0:T(8,128)S(1)}, u32[]{:S(2)}, u32[]{:S(2)}) collective-permute-start(f32[128,128]{1,0:T(8,128)S(1)} %add_add_fusion.refs_0_), channel_id=1, source_target_pairs={{0,4},{1,5},{2,6},{3,7},{4,0},{5,1},{6,2},{7,3},{8,12},{9,13},{10,... | collective-permute-start | bytes 196616 | tf_op jit(solution)/shard_map/ppermute | solution.py:136
  51.3 4.3 %collective-permute-start.15 = (f32[128,128]{1,0:T(8,128)S(1)}, f32[128,128]{1,0:T(8,128)S(1)}, u32[]{:S(2)}, u32[]{:S(2)}) collective-permute-start(f32[128,128]{1,0:T(8,128)S(1)} %add_add_fusion.refs_0_), channel_id=1, source_target_pairs={{0,2},{1,3},{2,0},{3,1},{4,6},{5,7},{6,4},{7,5},{8,10},{9,11},{10,... | collective-permute-start | bytes 196616 | tf_op jit(solution)/shard_map/ppermute | solution.py:136
  51.8 8.7 %collective-permute-start.18 = (f32[128,128]{1,0:T(8,128)S(1)}, f32[128,128]{1,0:T(8,128)S(1)}, u32[]{:S(2)}, u32[]{:S(2)}) collective-permute-start(f32[128,128]{1,0:T(8,128)S(1)} %add_add_fusion.refs_0_), channel_id=1, source_target_pairs={{0,1},{1,0},{2,3},{3,2},{4,5},{5,4},{6,7},{7,6},{8,9},{9,8},{10,11... | collective-permute-start | bytes 196616 | tf_op jit(solution)/shard_map/ppermute | solution.py:126
  53.5 7.0 %collective-permute-start.21 = (f32[128,128]{1,0:T(8,128)S(1)}, f32[128,128]{1,0:T(8,128)S(1)}, u32[]{:S(2)}, u32[]{:S(2)}) collective-permute-start(f32[128,128]{1,0:T(8,128)S(1)} %collective-permute-done.17.refs_3_), channel_id=1, source_target_pairs={{0,1},{1,0},{2,3},{3,2},{4,5},{5,4},{6,7},{7,6},{8,9},{9,8},{10,11... | collective-permute-start | bytes 196616 | tf_op jit(solution)/shard_map/ppermute | solution.py:126
  54.3 6.3 %collective-permute-start.20 = (f32[128,128]{1,0:T(8,128)S(1)}, f32[128,128]{1,0:T(8,128)S(1)}, u32[]{:S(2)}, u32[]{:S(2)}) collective-permute-start(f32[128,128]{1,0:T(8,128)S(1)} %collective-permute-done.16.refs_2_), channel_id=1, source_target_pairs={{0,1},{1,0},{2,3},{3,2},{4,5},{5,4},{6,7},{7,6},{8,9},{9,8},{10,11... | collective-permute-start | bytes 196616 | tf_op jit(solution)/shard_map/ppermute | solution.py:126
  55.6 4.9 %collective-permute-start.19 = (f32[128,128]{1,0:T(8,128)S(1)}, f32[128,128]{1,0:T(8,128)S(1)}, u32[]{:S(2)}, u32[]{:S(2)}) collective-permute-start(f32[128,128]{1,0:T(8,128)S(1)} %collective-permute-done.15.refs_1_), channel_id=1, source_target_pairs={{0,1},{1,0},{2,3},{3,2},{4,5},{5,4},{6,7},{7,6},{8,9},{9,8},{10,11... | collective-permute-start | bytes 196616 | tf_op jit(solution)/shard_map/ppermute | solution.py:126
  55.6 4.9 %collective-permute-start.22 = (f32[64,128]{1,0:T(8,128)S(1)}, f32[64,128]{1,0:T(8,128)S(1)}, u32[]{:S(2)}, u32[]{:S(2)}) collective-permute-start(f32[64,128]{1,0:T(8,128)S(1)} %get-tuple-element.32.refs_8_), channel_id=1, source_target_pairs={{0,16},{8,24},{16,0},{24,8},{1,17},{9,25},{17,1},{25,9},{2,18},{10... | collective-permute-start | bytes 98312 | tf_op jit(solution)/shard_map/ppermute | solution.py:126

commit v2 on v1

--- a/solution.py
+++ b/solution.py
@@ -392,7 +392,10 @@
     eye_lane = lax.broadcasted_iota(jnp.int32, (vecs, vecs), 1)
     error = split_dot(basis, basis, across) - (eye_sub == eye_lane).astype(f32)
     weight = jnp.where(eye_sub > eye_lane, 1.0, jnp.where(eye_sub == eye_lane, 0.5, 0.0))
-    wide_ref[...] = (basis - split_dot(error * weight, basis)) * math.sqrt(snaps)
+    fix = jnp.dot(
+        (error * weight).astype(bf16), basis.astype(bf16), preferred_element_type=f32
+    )
+    wide_ref[...] = (basis - fix) * math.sqrt(snaps)
     out_ref[...] = wide_ref[:, pl.ds(pl.multiple_of(row_place * rows, TILE), rows)]
 
 

time: 66 us -> 65.9 us (level)
  no operation moved by 1% of the time
where the time goes in v2:
time: 65.9 us; the launch traced here: 65.7 us
  starting transfers between devices  30.6 us (46%)
  waiting for transfers between devices  25.3 us (38%)
  Pallas kernels  9.7 us (15%)
    ppermute x7, starting transfers between devices, packed_plan(): received.append(lax.ppermute(cuts[step], ('row', 'col'), pairs))  17.2 us
    ppermute x10, waiting for transfers between devices, xor_permute(): lax.ppermute(x, axis, [(i, i ^ mask) for i in range(lax.axis_size(axis))])  11.9 us
    ppermute x6, starting transfers between devices, quad_permute(): return lax.ppermute(x, ('col', 'feat'), pairs)  7.11 us
    ppermute x6, waiting for transfers between devices, quad_permute(): return lax.ppermute(x, ('col', 'feat'), pairs)  6.74 us
    ppermute x7, waiting for transfers between devices, packed_plan(): received.append(lax.ppermute(cuts[step], ('row', 'col'), pairs))  6.65 us
    ppermute x10, starting transfers between devices, xor_permute(): lax.ppermute(x, axis, [(i, i ^ mask) for i in range(lax.axis_size(axis))])  6.28 us
    pallas_call x1, Pallas kernels, packed_plan(): pl.pallas_call(functools.partial(finish_kernel, float(points), tiles, chu...  5.17 us
    pallas_call x1, Pallas kernels, packed_plan(): pl.pallas_call(functools.partial(gram_kernel, steps, rows_total, cols, sh...  2.36 us
  transfers between devices with their start and end apart: 23, of which 11 were waited for; matrix products, arithmetic and copies ran while one was open for 0% of the time, Pallas kernels for 2%

profile of v2, /device:TPU:0, one launch (start us, length us, event | category | flops | bytes accessed | tf_op | source)
XLA Modules:
  0.0 65.7 jit_solution(15974015469677929685)
XLA Ops:
  0.0 0.8 %cut.3 = bf16[64,1024]{1,0:T(8,128)(2,1)S(1)} custom-call(bf16[64,8192]{1,0:T(8,128)(2,1)} %x_ref.3), custom_call_target="tpu_custom_call" | custom-call | tf_op jit(solution)/shard_map/cut/pallas_call | solution.py:419
  0.8 0.0 copy-start
  0.9 4.1 %collective-permute-start = (bf16[64,1024]{1,0:T(8,128)(2,1)S(1)}, bf16[64,1024]{1,0:T(8,128)(2,1)S(1)}, u32[]{:S(2)}, u32[]{:S(2)}) collective-permute-start(bf16[64,1024]{1,0:T(8,128)(2,1)S(1)} %cut.3), channel_id=1, source_target_pairs={{0,16},{4,20},{8,24},{12,28},{16,0},{20,4},{24,8},{28,12},{1,17},{... | collective-permute-start | bytes 393224 | tf_op jit(solution)/shard_map/ppermute | solution.py:436
  5.0 1.3 %cut.2 = (bf16[64,1024]{1,0:T(8,128)(2,1)S(1)}, bf16[64,1024]{1,0:T(8,128)(2,1)S(1)}, bf16[64,1024]{1,0:T(8,128)(2,1)S(1)}, bf16[64,1024]{1,0:T(8,128)(2,1)S(1)}...) custom-call(bf16[64,8192]{1,0:T(8,128)(2,1)} %x_ref.3), custom_call_target="tpu_custom_call" | custom-call | tf_op jit(solution)/shard_map/cut/pallas_call | solution.py:419
  6.3 2.6 %collective-permute-start.1 = (bf16[64,1024]{1,0:T(8,128)(2,1)S(1)}, bf16[64,1024]{1,0:T(8,128)(2,1)S(1)}, u32[]{:S(2)}, u32[]{:S(2)}) collective-permute-start(bf16[64,1024]{1,0:T(8,128)(2,1)S(1)} %get-tuple-element.20), channel_id=1, source_target_pairs={{0,12},{4,8},{8,20},{12,16},{16,28},{20,24},{24,4},{28,0},{1,13},{... | collective-permute-start | bytes 393224 | tf_op jit(solution)/shard_map/ppermute | solution.py:436
  8.9 0.0 copy-done
  8.9 0.0 collective-permute-start.7
  8.9 2.2 %collective-permute-start.2 = (bf16[64,1024]{1,0:T(8,128)(2,1)S(1)}, bf16[64,1024]{1,0:T(8,128)(2,1)S(1)}, u32[]{:S(2)}, u32[]{:S(2)}) collective-permute-start(bf16[64,1024]{1,0:T(8,128)(2,1)S(1)} %get-tuple-element.21), channel_id=1, source_target_pairs={{0,24},{4,28},{8,0},{12,4},{16,8},{20,12},{24,16},{28,20},{1,25},{... | collective-permute-start | bytes 393224 | tf_op jit(solution)/shard_map/ppermute | solution.py:436
  11.1 1.2 %collective-permute-start.3 = (bf16[64,1024]{1,0:T(8,128)(2,1)S(1)}, bf16[64,1024]{1,0:T(8,128)(2,1)S(1)}, u32[]{:S(2)}, u32[]{:S(2)}) collective-permute-start(bf16[64,1024]{1,0:T(8,128)(2,1)S(1)} %get-tuple-element.22), channel_id=1, source_target_pairs={{0,20},{4,16},{8,28},{12,24},{16,4},{20,0},{24,12},{28,8},{1,21},{... | collective-permute-start | bytes 393224 | tf_op jit(solution)/shard_map/ppermute | solution.py:436
  12.3 1.3 %collective-permute-done.7.refs_9_ = f32[32,128]{1,0:T(8,128)S(1)} collective-permute-done((f32[32,128]{1,0:T(8,128)S(1)}, f32[32,128]{1,0:T(8,128)S(1)}, u32[]{:S(2)}, u32[]{:S(2)}) %collective-permute-start.7) | collective-permute-done | bytes 16416 | tf_op jit(solution)/shard_map/ppermute | solution.py:126
  13.6 1.7 %collective-permute-start.4 = (bf16[64,1024]{1,0:T(8,128)(2,1)S(1)}, bf16[64,1024]{1,0:T(8,128)(2,1)S(1)}, u32[]{:S(2)}, u32[]{:S(2)}) collective-permute-start(bf16[64,1024]{1,0:T(8,128)(2,1)S(1)} %get-tuple-element.23), channel_id=1, source_target_pairs={{0,8},{4,12},{8,16},{12,20},{16,24},{20,28},{24,0},{28,4},{1,9},{5... | collective-permute-start | bytes 393224 | tf_op jit(solution)/shard_map/ppermute | solution.py:436
  15.4 0.0 collective-permute-done.refs_1_
  15.4 3.4 %collective-permute-start.5 = (bf16[64,1024]{1,0:T(8,128)(2,1)S(1)}, bf16[64,1024]{1,0:T(8,128)(2,1)S(1)}, u32[]{:S(2)}, u32[]{:S(2)}) collective-permute-start(bf16[64,1024]{1,0:T(8,128)(2,1)S(1)} %get-tuple-element.24), channel_id=1, source_target_pairs={{0,28},{4,24},{8,4},{12,0},{16,12},{20,8},{24,20},{28,16},{1,29},{... | collective-permute-start | bytes 393224 | tf_op jit(solution)/shard_map/ppermute | solution.py:436
  18.7 0.0 collective-permute-done.1.refs_2_
  18.7 2.0 %collective-permute-start.6 = (bf16[64,1024]{1,0:T(8,128)(2,1)S(1)}, bf16[64,1024]{1,0:T(8,128)(2,1)S(1)}, u32[]{:S(2)}, u32[]{:S(2)}) collective-permute-start(bf16[64,1024]{1,0:T(8,128)(2,1)S(1)} %get-tuple-element.25), channel_id=1, source_target_pairs={{0,4},{4,0},{8,12},{12,8},{16,20},{20,16},{24,28},{28,24},{1,5},{5... | collective-permute-start | bytes 393224 | tf_op jit(solution)/shard_map/ppermute | solution.py:436
  20.7 0.0 collective-permute-done.2.refs_3_
  20.7 6.6 %collective-permute-done.3.refs_4_ = bf16[64,1024]{1,0:T(8,128)(2,1)S(1)} collective-permute-done((bf16[64,1024]{1,0:T(8,128)(2,1)S(1)}, bf16[64,1024]{1,0:T(8,128)(2,1)S(1)}, u32[]{:S(2)}, u32[]{:S(2)}) %collective-permute-start.3) | collective-permute-done | bytes 131104 | tf_op jit(solution)/shard_map/ppermute | solution.py:436
  27.3 0.0 collective-permute-done.4.refs_5_
  27.3 0.0 collective-permute-done.5.refs_6_
  27.3 0.0 collective-permute-done.6.refs_7_
  27.3 2.4 %gram.1 = (f32[512,128]{1,0:T(8,128)S(1)}, f32[512,128]{1,0:T(8,128)S(1)}, f32[64,128]{1,0:T(8,128)S(1)}) custom-call(bf16[64,1024]{1,0:T(8,128)(2,1)S(1)} %get-tuple-element.19.refs_0_, bf16[64,1024]{1,0:T(8,128)(2,1)S(1)} %collective-permute-done.refs_1_, bf16[64,1024]{1,0:T(8,128)(2,1)S(1)} %collective-permute-done.1.refs_2_, ...), custom_call_target="tpu_custom_call" | custom-call | tf_op jit(solution)/shard_map/gram/pallas_call | solution.py:444
  29.7 0.1 collective-permute-start.8
  29.8 1.5 %collective-permute-done.8.got_ref = f32[512,128]{1,0:T(8,128)S(1)} collective-permute-done((f32[512,128]{1,0:T(8,128)S(1)}, f32[512,128]{1,0:T(8,128)S(1)}, u32[]{:S(2)}, u32[]{:S(2)}) %collective-permute-start.8) | collective-permute-done | bytes 262176 | tf_op jit(solution)/shard_map/ppermute | solution.py:126
  31.3 1.8 %collective-permute-start.9 = (f32[128,128]{1,0:T(8,128)S(1)}, f32[128,128]{1,0:T(8,128)S(1)}, u32[]{:S(2)}, u32[]{:S(2)}) collective-permute-start(f32[128,128]{1,0:T(8,128)S(1)} %get-tuple-element.29), channel_id=1, source_target_pairs={{0,6},{1,7},{2,4},{3,5},{4,2},{5,3},{6,0},{7,1},{8,14},{9,15},{10,... | collective-permute-start | bytes 196616 | tf_op jit(solution)/shard_map/ppermute | solution.py:136
  33.1 0.4 collective-permute-start.10
  33.5 1.4 %collective-permute-start.11 = (f32[128,128]{1,0:T(8,128)S(1)}, f32[128,128]{1,0:T(8,128)S(1)}, u32[]{:S(2)}, u32[]{:S(2)}) collective-permute-start(f32[128,128]{1,0:T(8,128)S(1)} %get-tuple-element.31), channel_id=1, source_target_pairs={{0,4},{1,5},{2,6},{3,7},{4,0},{5,1},{6,2},{7,3},{8,12},{9,13},{10,... | collective-permute-start | bytes 196616 | tf_op jit(solution)/shard_map/ppermute | solution.py:136
  34.9 1.7 %collective-permute-done.9 = f32[128,128]{1,0:T(8,128)S(1)} collective-permute-done((f32[128,128]{1,0:T(8,128)S(1)}, f32[128,128]{1,0:T(8,128)S(1)}, u32[]{:S(2)}, u32[]{:S(2)}) %collective-permute-start.9) | collective-permute-done | bytes 65568 | tf_op jit(solution)/shard_map/ppermute | solution.py:136
  36.6 1.3 %collective-permute-done.10 = f32[128,128]{1,0:T(8,128)S(1)} collective-permute-done((f32[128,128]{1,0:T(8,128)S(1)}, f32[128,128]{1,0:T(8,128)S(1)}, u32[]{:S(2)}, u32[]{:S(2)}) %collective-permute-start.10) | collective-permute-done | bytes 65568 | tf_op jit(solution)/shard_map/ppermute | solution.py:136
  37.8 0.0 collective-permute-done.11
  37.9 4.3 %collective-permute-start.14 = (f32[128,128]{1,0:T(8,128)S(1)}, f32[128,128]{1,0:T(8,128)S(1)}, u32[]{:S(2)}, u32[]{:S(2)}) collective-permute-start(f32[128,128]{1,0:T(8,128)S(1)} %add_add_fusion.1), channel_id=1, source_target_pairs={{0,16},{8,24},{16,0},{24,8},{1,17},{9,25},{17,1},{25,9},{2,18},{10... | collective-permute-start | bytes 196616 | tf_op jit(solution)/shard_map/ppermute | solution.py:126
  42.2 0.5 collective-permute-start.13
  42.7 0.1 collective-permute-start.12
  42.8 3.9 %collective-permute-done.14 = f32[128,128]{1,0:T(8,128)S(1)} collective-permute-done((f32[128,128]{1,0:T(8,128)S(1)}, f32[128,128]{1,0:T(8,128)S(1)}, u32[]{:S(2)}, u32[]{:S(2)}) %collective-permute-start.14) | collective-permute-done | bytes 65568 | tf_op jit(solution)/shard_map/ppermute | solution.py:126
  46.7 1.6 %collective-permute-done.13 = f32[128,128]{1,0:T(8,128)S(1)} collective-permute-done((f32[128,128]{1,0:T(8,128)S(1)}, f32[128,128]{1,0:T(8,128)S(1)}, u32[]{:S(2)}, u32[]{:S(2)}) %collective-permute-start.13) | collective-permute-done | bytes 65568 | tf_op jit(solution)/shard_map/ppermute | solution.py:126
  48.3 0.0 collective-permute-done.12
  48.3 1.7 %collective-permute-start.17 = (f32[128,128]{1,0:T(8,128)S(1)}, f32[128,128]{1,0:T(8,128)S(1)}, u32[]{:S(2)}, u32[]{:S(2)}) collective-permute-start(f32[128,128]{1,0:T(8,128)S(1)} %add_add_fusion.refs_0_), channel_id=1, source_target_pairs={{0,6},{1,7},{2,4},{3,5},{4,2},{5,3},{6,0},{7,1},{8,14},{9,15},{10,... | collective-permute-start | bytes 196616 | tf_op jit(solution)/shard_map/ppermute | solution.py:136
  50.0 1.3 %collective-permute-start.16 = (f32[128,128]{1,0:T(8,128)S(1)}, f32[128,128]{1,0:T(8,128)S(1)}, u32[]{:S(2)}, u32[]{:S(2)}) collective-permute-start(f32[128,128]{1,0:T(8,128)S(1)} %add_add_fusion.refs_0_), channel_id=1, source_target_pairs={{0,4},{1,5},{2,6},{3,7},{4,0},{5,1},{6,2},{7,3},{8,12},{9,13},{10,... | collective-permute-start | bytes 196616 | tf_op jit(solution)/shard_map/ppermute | solution.py:136
  51.3 0.5 collective-permute-start.15
  51.8 0.0 collective-permute-start.18
  51.8 1.7 %collective-permute-done.17.refs_3_ = f32[128,128]{1,0:T(8,128)S(1)} collective-permute-done((f32[128,128]{1,0:T(8,128)S(1)}, f32[128,128]{1,0:T(8,128)S(1)}, u32[]{:S(2)}, u32[]{:S(2)}) %collective-permute-start.17) | collective-permute-done | bytes 65568 | tf_op jit(solution)/shard_map/ppermute | solution.py:136
  53.5 0.0 collective-permute-start.21
  53.5 0.8 %collective-permute-done.16.refs_2_ = f32[128,128]{1,0:T(8,128)S(1)} collective-permute-done((f32[128,128]{1,0:T(8,128)S(1)}, f32[128,128]{1,0:T(8,128)S(1)}, u32[]{:S(2)}, u32[]{:S(2)}) %collective-permute-start.16) | collective-permute-done | bytes 65568 | tf_op jit(solution)/shard_map/ppermute | solution.py:136
  54.3 0.0 collective-permute-start.20
  54.3 1.3 %collective-permute-done.15.refs_1_ = f32[128,128]{1,0:T(8,128)S(1)} collective-permute-done((f32[128,128]{1,0:T(8,128)S(1)}, f32[128,128]{1,0:T(8,128)S(1)}, u32[]{:S(2)}, u32[]{:S(2)}) %collective-permute-start.15) | collective-permute-done | bytes 65568 | tf_op jit(solution)/shard_map/ppermute | solution.py:136
  55.6 0.0 collective-permute-start.19
  55.6 1.3 %collective-permute-start.22 = (f32[64,128]{1,0:T(8,128)S(1)}, f32[64,128]{1,0:T(8,128)S(1)}, u32[]{:S(2)}, u32[]{:S(2)}) collective-permute-start(f32[64,128]{1,0:T(8,128)S(1)} %get-tuple-element.32.refs_8_), channel_id=1, source_target_pairs={{0,16},{8,24},{16,0},{24,8},{1,17},{9,25},{17,1},{25,9},{2,18},{10... | collective-permute-start | bytes 98312 | tf_op jit(solution)/shard_map/ppermute | solution.py:126
  56.9 3.7 %collective-permute-done.22.refs_9_ = f32[64,128]{1,0:T(8,128)S(1)} collective-permute-done((f32[64,128]{1,0:T(8,128)S(1)}, f32[64,128]{1,0:T(8,128)S(1)}, u32[]{:S(2)}, u32[]{:S(2)}) %collective-permute-start.22) | collective-permute-done | bytes 32800 | tf_op jit(solution)/shard_map/ppermute | solution.py:126
  60.5 0.0 collective-permute-done.18.refs_4_
  60.5 0.0 collective-permute-done.21.refs_7_
  60.5 0.0 collective-permute-done.20.refs_6_
  60.5 0.0 collective-permute-done.19.refs_5_
  60.5 5.2 %finish.1 = f32[32,128]{1,0:T(8,128)} custom-call(f32[128,128]{1,0:T(8,128)S(1)} %add_add_fusion.refs_0_, f32[128,128]{1,0:T(8,128)S(1)} %collective-permute-done.15.refs_1_, f32[128,128]{1,0:T(8,128)S(1)} %collective-permute-done.16.refs_2_, f32[128,128]{1,0:T(8,128)S(1)} %collective-permute-done.17.refs_3_, ...), custom_call_target="tpu_custom_call" | custom-call | tf_op jit(solution)/shard_map/finish/pallas_call | solution.py:470
  (3 shorter events, 0.1 us)
Async XLA Ops:
  0.8 8.0 %copy-start = (f32[128,32]{0,1:T(8,128)S(1)}, f32[128,32]{0,1:T(8,128)}, u32[]{:S(2)}) copy-start(f32[128,32]{0,1:T(8,128)} %param.3) | copy-start | bytes 49156
  0.9 14.5 %collective-permute-start = (bf16[64,1024]{1,0:T(8,128)(2,1)S(1)}, bf16[64,1024]{1,0:T(8,128)(2,1)S(1)}, u32[]{:S(2)}, u32[]{:S(2)}) collective-permute-start(bf16[64,1024]{1,0:T(8,128)(2,1)S(1)} %cut.3), channel_id=1, source_target_pairs={{0,16},{4,20},{8,24},{12,28},{16,0},{20,4},{24,8},{28,12},{1,17},{... | collective-permute-start | bytes 393224 | tf_op jit(solution)/shard_map/ppermute | solution.py:436
  6.3 12.4 %collective-permute-start.1 = (bf16[64,1024]{1,0:T(8,128)(2,1)S(1)}, bf16[64,1024]{1,0:T(8,128)(2,1)S(1)}, u32[]{:S(2)}, u32[]{:S(2)}) collective-permute-start(bf16[64,1024]{1,0:T(8,128)(2,1)S(1)} %get-tuple-element.20), channel_id=1, source_target_pairs={{0,12},{4,8},{8,20},{12,16},{16,28},{20,24},{24,4},{28,0},{1,13},{... | collective-permute-start | bytes 393224 | tf_op jit(solution)/shard_map/ppermute | solution.py:436
  8.9 4.8 %collective-permute-start.7 = (f32[32,128]{1,0:T(8,128)S(1)}, f32[32,128]{1,0:T(8,128)S(1)}, u32[]{:S(2)}, u32[]{:S(2)}) collective-permute-start(f32[32,128]{1,0:T(8,128)S(1)} %bitcast.2), channel_id=1, source_target_pairs={{0,8},{8,0},{16,24},{24,16},{1,9},{9,1},{17,25},{25,17},{2,10},{10... | collective-permute-start | bytes 49160 | tf_op jit(solution)/shard_map/ppermute | solution.py:126
  8.9 11.8 %collective-permute-start.2 = (bf16[64,1024]{1,0:T(8,128)(2,1)S(1)}, bf16[64,1024]{1,0:T(8,128)(2,1)S(1)}, u32[]{:S(2)}, u32[]{:S(2)}) collective-permute-start(bf16[64,1024]{1,0:T(8,128)(2,1)S(1)} %get-tuple-element.21), channel_id=1, source_target_pairs={{0,24},{4,28},{8,0},{12,4},{16,8},{20,12},{24,16},{28,20},{1,25},{... | collective-permute-start | bytes 393224 | tf_op jit(solution)/shard_map/ppermute | solution.py:436
  11.1 16.2 %collective-permute-start.3 = (bf16[64,1024]{1,0:T(8,128)(2,1)S(1)}, bf16[64,1024]{1,0:T(8,128)(2,1)S(1)}, u32[]{:S(2)}, u32[]{:S(2)}) collective-permute-start(bf16[64,1024]{1,0:T(8,128)(2,1)S(1)} %get-tuple-element.22), channel_id=1, source_target_pairs={{0,20},{4,16},{8,28},{12,24},{16,4},{20,0},{24,12},{28,8},{1,21},{... | collective-permute-start | bytes 393224 | tf_op jit(solution)/shard_map/ppermute | solution.py:436
  13.6 13.7 %collective-permute-start.4 = (bf16[64,1024]{1,0:T(8,128)(2,1)S(1)}, bf16[64,1024]{1,0:T(8,128)(2,1)S(1)}, u32[]{:S(2)}, u32[]{:S(2)}) collective-permute-start(bf16[64,1024]{1,0:T(8,128)(2,1)S(1)} %get-tuple-element.23), channel_id=1, source_target_pairs={{0,8},{4,12},{8,16},{12,20},{16,24},{20,28},{24,0},{28,4},{1,9},{5... | collective-permute-start | bytes 393224 | tf_op jit(solution)/shard_map/ppermute | solution.py:436
  15.4 12.0 %collective-permute-start.5 = (bf16[64,1024]{1,0:T(8,128)(2,1)S(1)}, bf16[64,1024]{1,0:T(8,128)(2,1)S(1)}, u32[]{:S(2)}, u32[]{:S(2)}) collective-permute-start(bf16[64,1024]{1,0:T(8,128)(2,1)S(1)} %get-tuple-element.24), channel_id=1, source_target_pairs={{0,28},{4,24},{8,4},{12,0},{16,12},{20,8},{24,20},{28,16},{1,29},{... | collective-permute-start | bytes 393224 | tf_op jit(solution)/shard_map/ppermute | solution.py:436
  18.7 8.6 %collective-permute-start.6 = (bf16[64,1024]{1,0:T(8,128)(2,1)S(1)}, bf16[64,1024]{1,0:T(8,128)(2,1)S(1)}, u32[]{:S(2)}, u32[]{:S(2)}) collective-permute-start(bf16[64,1024]{1,0:T(8,128)(2,1)S(1)} %get-tuple-element.25), channel_id=1, source_target_pairs={{0,4},{4,0},{8,12},{12,8},{16,20},{20,16},{24,28},{28,24},{1,5},{5... | collective-permute-start | bytes 393224 | tf_op jit(solution)/shard_map/ppermute | solution.py:436
  29.7 1.6 %collective-permute-start.8 = (f32[512,128]{1,0:T(8,128)S(1)}, f32[512,128]{1,0:T(8,128)S(1)}, u32[]{:S(2)}, u32[]{:S(2)}) collective-permute-start(f32[512,128]{1,0:T(8,128)S(1)} %get-tuple-element.27), channel_id=1, source_target_pairs={{0,1},{1,0},{2,3},{3,2},{4,5},{5,4},{6,7},{7,6},{8,9},{9,8},{10,11... | collective-permute-start | bytes 786440 | tf_op jit(solution)/shard_map/ppermute | solution.py:126
  31.3 5.2 %collective-permute-start.9 = (f32[128,128]{1,0:T(8,128)S(1)}, f32[128,128]{1,0:T(8,128)S(1)}, u32[]{:S(2)}, u32[]{:S(2)}) collective-permute-start(f32[128,128]{1,0:T(8,128)S(1)} %get-tuple-element.29), channel_id=1, source_target_pairs={{0,6},{1,7},{2,4},{3,5},{4,2},{5,3},{6,0},{7,1},{8,14},{9,15},{10,... | collective-permute-start | bytes 196616 | tf_op jit(solution)/shard_map/ppermute | solution.py:136
  33.1 4.7 %collective-permute-start.10 = (f32[128,128]{1,0:T(8,128)S(1)}, f32[128,128]{1,0:T(8,128)S(1)}, u32[]{:S(2)}, u32[]{:S(2)}) collective-permute-start(f32[128,128]{1,0:T(8,128)S(1)} %get-tuple-element.30), channel_id=1, source_target_pairs={{0,2},{1,3},{2,0},{3,1},{4,6},{5,7},{6,4},{7,5},{8,10},{9,11},{10,... | collective-permute-start | bytes 196616 | tf_op jit(solution)/shard_map/ppermute | solution.py:136
  33.5 4.4 %collective-permute-start.11 = (f32[128,128]{1,0:T(8,128)S(1)}, f32[128,128]{1,0:T(8,128)S(1)}, u32[]{:S(2)}, u32[]{:S(2)}) collective-permute-start(f32[128,128]{1,0:T(8,128)S(1)} %get-tuple-element.31), channel_id=1, source_target_pairs={{0,4},{1,5},{2,6},{3,7},{4,0},{5,1},{6,2},{7,3},{8,12},{9,13},{10,... | collective-permute-start | bytes 196616 | tf_op jit(solution)/shard_map/ppermute | solution.py:136
  37.9 8.8 %collective-permute-start.14 = (f32[128,128]{1,0:T(8,128)S(1)}, f32[128,128]{1,0:T(8,128)S(1)}, u32[]{:S(2)}, u32[]{:S(2)}) collective-permute-start(f32[128,128]{1,0:T(8,128)S(1)} %add_add_fusion.1), channel_id=1, source_target_pairs={{0,16},{8,24},{16,0},{24,8},{1,17},{9,25},{17,1},{25,9},{2,18},{10... | collective-permute-start | bytes 196616 | tf_op jit(solution)/shard_map/ppermute | solution.py:126
  42.2 6.1 %collective-permute-start.13 = (f32[128,128]{1,0:T(8,128)S(1)}, f32[128,128]{1,0:T(8,128)S(1)}, u32[]{:S(2)}, u32[]{:S(2)}) collective-permute-start(f32[128,128]{1,0:T(8,128)S(1)} %add_add_fusion.1), channel_id=1, source_target_pairs={{0,24},{8,16},{16,8},{24,0},{1,25},{9,17},{17,9},{25,1},{2,26},{10... | collective-permute-start | bytes 196616 | tf_op jit(solution)/shard_map/ppermute | solution.py:126
  42.7 5.5 %collective-permute-start.12 = (f32[128,128]{1,0:T(8,128)S(1)}, f32[128,128]{1,0:T(8,128)S(1)}, u32[]{:S(2)}, u32[]{:S(2)}) collective-permute-start(f32[128,128]{1,0:T(8,128)S(1)} %add_add_fusion.1), channel_id=1, source_target_pairs={{0,8},{8,0},{16,24},{24,16},{1,9},{9,1},{17,25},{25,17},{2,10},{10... | collective-permute-start | bytes 196616 | tf_op jit(solution)/shard_map/ppermute | solution.py:126
  48.3 5.2 %collective-permute-start.17 = (f32[128,128]{1,0:T(8,128)S(1)}, f32[128,128]{1,0:T(8,128)S(1)}, u32[]{:S(2)}, u32[]{:S(2)}) collective-permute-start(f32[128,128]{1,0:T(8,128)S(1)} %add_add_fusion.refs_0_), channel_id=1, source_target_pairs={{0,6},{1,7},{2,4},{3,5},{4,2},{5,3},{6,0},{7,1},{8,14},{9,15},{10,... | collective-permute-start | bytes 196616 | tf_op jit(solution)/shard_map/ppermute | solution.py:136
  50.0 4.3 %collective-permute-start.16 = (f32[128,128]{1,0:T(8,128)S(1)}, f32[128,128]{1,0:T(8,128)S(1)}, u32[]{:S(2)}, u32[]{:S(2)}) collective-permute-start(f32[128,128]{1,0:T(8,128)S(1)} %add_add_fusion.refs_0_), channel_id=1, source_target_pairs={{0,4},{1,5},{2,6},{3,7},{4,0},{5,1},{6,2},{7,3},{8,12},{9,13},{10,... | collective-permute-start | bytes 196616 | tf_op jit(solution)/shard_map/ppermute | solution.py:136
  51.3 4.3 %collective-permute-start.15 = (f32[128,128]{1,0:T(8,128)S(1)}, f32[128,128]{1,0:T(8,128)S(1)}, u32[]{:S(2)}, u32[]{:S(2)}) collective-permute-start(f32[128,128]{1,0:T(8,128)S(1)} %add_add_fusion.refs_0_), channel_id=1, source_target_pairs={{0,2},{1,3},{2,0},{3,1},{4,6},{5,7},{6,4},{7,5},{8,10},{9,11},{10,... | collective-permute-start | bytes 196616 | tf_op jit(solution)/shard_map/ppermute | solution.py:136
  51.8 8.7 %collective-permute-start.18 = (f32[128,128]{1,0:T(8,128)S(1)}, f32[128,128]{1,0:T(8,128)S(1)}, u32[]{:S(2)}, u32[]{:S(2)}) collective-permute-start(f32[128,128]{1,0:T(8,128)S(1)} %add_add_fusion.refs_0_), channel_id=1, source_target_pairs={{0,1},{1,0},{2,3},{3,2},{4,5},{5,4},{6,7},{7,6},{8,9},{9,8},{10,11... | collective-permute-start | bytes 196616 | tf_op jit(solution)/shard_map/ppermute | solution.py:126
  53.5 7.0 %collective-permute-start.21 = (f32[128,128]{1,0:T(8,128)S(1)}, f32[128,128]{1,0:T(8,128)S(1)}, u32[]{:S(2)}, u32[]{:S(2)}) collective-permute-start(f32[128,128]{1,0:T(8,128)S(1)} %collective-permute-done.17.refs_3_), channel_id=1, source_target_pairs={{0,1},{1,0},{2,3},{3,2},{4,5},{5,4},{6,7},{7,6},{8,9},{9,8},{10,11... | collective-permute-start | bytes 196616 | tf_op jit(solution)/shard_map/ppermute | solution.py:126
  54.3 6.3 %collective-permute-start.20 = (f32[128,128]{1,0:T(8,128)S(1)}, f32[128,128]{1,0:T(8,128)S(1)}, u32[]{:S(2)}, u32[]{:S(2)}) collective-permute-start(f32[128,128]{1,0:T(8,128)S(1)} %collective-permute-done.16.refs_2_), channel_id=1, source_target_pairs={{0,1},{1,0},{2,3},{3,2},{4,5},{5,4},{6,7},{7,6},{8,9},{9,8},{10,11... | collective-permute-start | bytes 196616 | tf_op jit(solution)/shard_map/ppermute | solution.py:126
  55.6 4.9 %collective-permute-start.19 = (f32[128,128]{1,0:T(8,128)S(1)}, f32[128,128]{1,0:T(8,128)S(1)}, u32[]{:S(2)}, u32[]{:S(2)}) collective-permute-start(f32[128,128]{1,0:T(8,128)S(1)} %collective-permute-done.15.refs_1_), channel_id=1, source_target_pairs={{0,1},{1,0},{2,3},{3,2},{4,5},{5,4},{6,7},{7,6},{8,9},{9,8},{10,11... | collective-permute-start | bytes 196616 | tf_op jit(solution)/shard_map/ppermute | solution.py:126
  55.6 4.9 %collective-permute-start.22 = (f32[64,128]{1,0:T(8,128)S(1)}, f32[64,128]{1,0:T(8,128)S(1)}, u32[]{:S(2)}, u32[]{:S(2)}) collective-permute-start(f32[64,128]{1,0:T(8,128)S(1)} %get-tuple-element.32.refs_8_), channel_id=1, source_target_pairs={{0,16},{8,24},{16,0},{24,8},{1,17},{9,25},{17,1},{25,9},{2,18},{10... | collective-permute-start | bytes 98312 | tf_op jit(solution)/shard_map/ppermute | solution.py:126
